TPU v7x, 256 devices: a whole 4x4x8 slice. The times are simulated.
256 devices in a mesh: replica: 8 (over z), tile: 32 (over y, x, core).
Axes of the slice: x: 4, y: 4, z: 8, core: 2. Of those that a mesh axis runs over, the one named last changes fastest.
Arguments:
- fields: bfloat16 [8, 64, 128, 8, 128], P('replica', None, 'tile'), may hold values from -6 to 6
- convolution_weight: bfloat16 [64, 1728], replicated, may hold values from -0.15625 to 0.15625
- convolution_bias: float32 [64], replicated, may hold values from -3 to 3
- query_owner: int32 [8, 4096, 1], P('replica', 'tile'), may hold values from 0 to 31; in each aligned block of 128 rows (0 to 127, 128 to 255, ..., all dimensions but the last counted through in order) at most 8 rows name the same one
- query_cell: int32 [8, 4096], P('replica', 'tile'), may hold values from 0 to 4095
- query_frac: float32 [8, 3, 4096], P('replica', None, 'tile'), may hold values from 0 to 1
- target: float32 [8, 5, 4096], P('replica', None, 'tile'), may hold values from -6 to 6
- w_latent: float32 [64, 512], replicated, may hold values from -3 to 3
- w_pos: float32 [3, 512], replicated, may hold values from -3.5 to 3.5
- bias_one: float32 [512], replicated, may hold values from -2 to 2
- w_mid: float32 [512, 512], replicated, may hold values from -0.5 to 0.5
- bias_two: float32 [512], replicated, may hold values from -2 to 2
- w_out: float32 [5, 512], replicated, may hold values from -0.25 to 0.25
- bias_out: float32 [5], replicated, may hold values from -3 to 3
Outputs:
- prediction: float32 [8, 5, 4096], P('replica', None, 'tile')
- grad_latent: float32 [64, 512], replicated
- grad_pos: float32 [3, 512], replicated
- grad_bias_one: float32 [512], replicated
- grad_mid: float32 [512, 512], replicated
- grad_bias_two: float32 [512], replicated
- grad_out: float32 [5, 512], replicated
- grad_bias_out: float32 [5], replicated
- loss: float32 [], replicated
Inputs may be any that keep to these rules, and one draw needn't show every extreme that they name: `query_owner`: among the query points of one device, no tile is named more than 8 times; in every draw some device names some tile exactly 8 times.
All inputs are finite; a program needn't handle non-finite values.
Results may differ from a plain program's by a relative error of at most 0.0009.
The roundings to bfloat16 on the way count: a program that leaves them out, or rounds other values in their place, can miss the bound.
Values may be sent and summed in bfloat16 or wider, within the bound.
A program may use at most 64 MiB of HBM per device.

v0:
```python
import functools
import math

import jax
import jax.numpy as jnp
from jax import lax
from jax.experimental import pallas as pl
from jax.experimental.pallas import tpu as pltpu
from jax.sharding import PartitionSpec as P

VISCOSITY = 0.05
DIFFUSIVITY = 0.05
RESIDUAL_WEIGHT = 0.5
GELU_SCALE = math.sqrt(2.0 / math.pi)

MESH = pl.DeviceIdType.MESH
PLANES = 10
f32 = jnp.float32
bf16 = jnp.bfloat16


def halves(x):
    high = x.astype(bf16)
    return high, (x - high.astype(f32)).astype(bf16)


def product(left, right, dims):
    left_high, left_low = left
    right_high, right_low = right

    def one(a, b):
        return lax.dot_general(a, b, (dims, ((), ())), preferred_element_type=f32)

    total = one(left_high, right_high) + one(left_high, right_low)
    if left_low is not None:
        total = total + one(left_low, right_high)
    return total


NN = ((1,), (0,))
NT = ((1,), (1,))
TN = ((0,), (0,))


def encode_part(place, refs, scratch):
    z, tile, n_tile = place
    fields_ref, weight_ref, conv_bias_ref, owner_ref, cell_ref, frac_ref = refs
    (
        halo, taps, latent, corner, asked, wanted, answer, answered,
        halo_send, halo_recv, ask_send, ask_recv, answer_send, answer_recv,
    ) = scratch
    slots = 256 // n_tile
    above, below = lax.rem(tile + 1, n_tile), lax.rem(tile + n_tile - 1, n_tile)
    others = [lax.rem(tile + step, n_tile) for step in range(1, n_tile)]

    def at_tile(index):
        return {"replica": z, "tile": index}

    def halo_copy(plane, slot, target):
        return pltpu.make_async_remote_copy(
            src_ref=fields_ref.at[plane],
            dst_ref=halo.at[slot],
            send_sem=halo_send.at[slot],
            recv_sem=halo_recv.at[slot],
            device_id=at_tile(target),
            device_id_type=MESH,
        )

    halo_copies = {
        0: halo_copy(2, 0, above),
        2: halo_copy(0, 2, below),
        1: halo_copy(3, 1, above),
        3: halo_copy(1, 3, below),
        4: halo_copy(2, 4, below),
    }
    for copy in halo_copies.values():
        copy.start()

    lane = lax.broadcasted_iota(jnp.int32, (128, 128), 1)
    row = lax.broadcasted_iota(jnp.int32, (128, 128), 0)
    eye = lane == row

    def as_column(values):
        return jnp.sum(jnp.where(eye, jnp.broadcast_to(values, (128, 128)), 0.0), axis=1, keepdims=True)

    owner_row = owner_ref[...].astype(f32)
    owner_column = as_column(owner_row)
    same = (jnp.broadcast_to(owner_row, (128, 128)) == jnp.broadcast_to(owner_column, (128, 128))).astype(f32)
    rank_row = jnp.sum(jnp.where(row < lane, same, 0.0), axis=0, keepdims=True)
    rank_column = jnp.sum(jnp.where(lane < row, same, 0.0), axis=1, keepdims=True)
    key_row = (owner_row * slots + rank_row).astype(jnp.int32)
    key_column = (owner_column * slots + rank_column).astype(jnp.int32)
    to_slots = (
        lax.broadcasted_iota(jnp.int32, (256, 128), 0) == jnp.broadcast_to(key_row, (256, 128))
    ).astype(f32).astype(bf16)
    from_slots = (
        lax.broadcasted_iota(jnp.int32, (128, 256), 1) == jnp.broadcast_to(key_column, (128, 256))
    ).astype(f32).astype(bf16)
    cell = cell_ref[...]
    fraction = frac_ref[...]
    listed = [(cell // 64).astype(f32), (cell % 64).astype(f32)]
    for d in range(3):
        rest = fraction[d : d + 1]
        for _ in range(3):
            part = rest.astype(bf16).astype(f32)
            listed.append(part)
            rest = rest - part
    listed.append(jnp.zeros((117, 128), f32))
    asking = lax.dot_general(
        to_slots, jnp.concatenate(listed, axis=0).astype(bf16), (NT, ((), ())), preferred_element_type=f32
    )
    wanted[...] = asking

    def exchange(source, target, send_sems, recv_sems):
        mine = pl.ds(pl.multiple_of(tile * slots, 8), slots)
        copies = []
        for step, index in enumerate(others):
            theirs = pl.ds(pl.multiple_of(index * slots, 8), slots)
            copy = pltpu.make_async_remote_copy(
                src_ref=source.at[theirs],
                dst_ref=target.at[mine],
                send_sem=send_sems.at[step],
                recv_sem=recv_sems.at[tile],
                device_id=at_tile(index),
                device_id_type=MESH,
            )
            copy.start()
            copies.append(copy)
        target[mine] = source[mine]

        def finish():
            for step, index in enumerate(others):
                theirs = pl.ds(pl.multiple_of(index * slots, 8), slots)
                copies[step].wait_send()
                pltpu.make_async_remote_copy(
                    src_ref=target.at[theirs],
                    dst_ref=target.at[theirs],
                    send_sem=send_sems.at[step],
                    recv_sem=recv_sems.at[index],
                    device_id=at_tile(index),
                    device_id_type=MESH,
                ).wait_recv()

        return finish

    asked_finish = exchange(wanted, asked, ask_send, ask_recv)

    def position_of(base, d, span):
        return as_column((base.astype(f32) + fraction[d : d + 1]) * (1.0 / span))

    position = [
        position_of(owner_ref[...] * 4 + cell // 1024, 0, 4 * n_tile),
        position_of(cell // 128 % 8, 1, 8),
        position_of(cell % 128, 2, 128),
    ]

    turned = jnp.transpose(weight_ref[...].astype(f32)).astype(bf16)
    for dx in range(3):
        for y_in in range(4):
            for dz in range(3):
                sides = []
                for y_out in range(2):
                    dy = y_in - y_out
                    if 0 <= dy <= 2:
                        tap = 9 * dx + 3 * dy + dz
                        sides.append(turned[tap * 64 : (tap + 1) * 64])
                    else:
                        sides.append(jnp.zeros((64, 64), bf16))
                taps[(dx * 4 + y_in) * 64 : (dx * 4 + y_in + 1) * 64, dz * 128 : (dz + 1) * 128] = (
                    jnp.concatenate(sides, axis=1)
                )

    asked_finish()
    table = asked[...]

    def spread(k):
        return jnp.broadcast_to(table[:, k : k + 1], (256, 128))

    cells = (64.0 * spread(0) + spread(1)).astype(jnp.int32)
    part = [spread(2 + 3 * d) + spread(3 + 3 * d) + spread(4 + 3 * d) for d in range(3)]
    base_x, base_y, base_z = cells // 1024, cells // 128 % 8, cells % 128
    lanes = lax.broadcasted_iota(jnp.int32, (256, 128), 1)
    zero = jnp.zeros((256, 128), f32)

    def side(base, index, span, fraction_part):
        high = jnp.where((base + 1) % span == index, fraction_part, zero)
        return jnp.where(base == index, 1.0 - fraction_part, high)

    weight_z = side(base_z, lanes, 128, part[2])
    weight_x = [side(base_x, p, 8, part[0]) for p in range(5)]
    for y in range(8):
        weight_y = side(base_y, y, 8, part[1])
        for p in range(5):
            start = (p * 4 + y // 2) * 128
            corner[y % 2, :, start : start + 128] = ((weight_x[p] * weight_y) * weight_z).astype(bf16)

    conv_bias = jnp.concatenate([conv_bias_ref[...], conv_bias_ref[...]], axis=1)
    arrived = set()

    def plane_pair(x, pair):
        columns = slice(pair * 128, (pair + 1) * 128)
        if 0 <= x < 4:
            return fields_ref[x][:, columns]
        slot = x + 2 if x < 0 else x - 2
        if slot not in arrived:
            arrived.add(slot)
            halo_copies[slot].wait()
        return halo[slot][:, columns]

    for p in (2, 0, 1, 3, 4):
        for pair in range(4):
            left = jnp.concatenate(
                [plane_pair(p + 2 * dx, (pair + k) % 4) for dx in (-1, 0, 1) for k in (0, 1)], axis=1
            )
            mixed = jnp.dot(left, taps[...], preferred_element_type=f32)
            v = (
                mixed[:, 128:256]
                + pltpu.roll(mixed[:, 0:128], 1, axis=0)
                + pltpu.roll(mixed[:, 256:384], 127, axis=0)
                + conv_bias
            )
            v = 0.5 * v * (1.0 + jnp.tanh(GELU_SCALE * (v + 0.044715 * (v * v * v))))
            latent[(p * 4 + pair) * 128 : (p * 4 + pair + 1) * 128] = v.astype(bf16)

    even = jnp.dot(corner[0], latent[...], preferred_element_type=f32)
    odd = jnp.dot(corner[1], latent[...], preferred_element_type=f32)
    answer[...] = (even + pltpu.roll(odd, 64, axis=1)).astype(bf16).astype(f32)
    exchange(answer, answered, answer_send, answer_recv)()
    interp = jnp.dot(from_slots, answered[...].astype(bf16), preferred_element_type=f32)
    return interp[:, :64].astype(bf16), position


def step_kernel(
    sizes,
    fields_ref, weight_ref, conv_bias_ref, owner_ref, cell_ref, frac_ref,
    target_ref, w_latent_ref, w_pos_ref, bias_one_ref, w_mid_ref,
    bias_two_ref, w_out_ref, bias_out_ref,
    prediction_ref, packed_ref,
    grads, pair_buf, plane_buf, z_send, z_buf, z_all, piece,
    act_high, act_low, cot_high, cot_low,
    pair_send, pair_recv, plane_send, plane_recv, zs_send, zs_recv, zg_send, zg_recv,
    pg_send, pg_recv, cg_send, cg_recv,
    *encode_scratch,
):
    n_z, n_tile, query_total = sizes
    n_xy = n_tile // 2
    rows_xy = 128 // n_xy
    rows_z = rows_xy // n_z
    z = lax.axis_index("replica")
    tile = lax.axis_index("tile")
    core = lax.rem(tile, 2)
    chip = tile // 2
    other = 1 - core

    def at_tile(chip_index, core_index):
        return {"replica": z, "tile": chip_index * 2 + core_index}

    def at_z(z_index):
        return {"replica": z_index, "tile": tile}

    chips = [lax.rem(chip + step, n_xy) for step in range(1, n_xy)]
    depths = [lax.rem(z + step, n_z) for step in range(1, n_z)]
    barrier = pltpu.get_barrier_semaphore()
    for step in range(1, n_tile):
        pl.semaphore_signal(
            barrier, inc=1, device_id={"replica": z, "tile": lax.rem(tile + step, n_tile)}, device_id_type=MESH
        )
    for z_index in depths:
        pl.semaphore_signal(barrier, inc=1, device_id=at_z(z_index), device_id_type=MESH)
    pl.semaphore_wait(barrier, n_tile + n_z - 2)
    latent_rows, position = encode_part(
        (z, tile, n_tile),
        (fields_ref, weight_ref, conv_bias_ref, owner_ref, cell_ref, frac_ref),
        encode_scratch,
    )

    w_pos = w_pos_ref[...]
    first_sum = product((latent_rows, None), halves(w_latent_ref[...]), NN) + bias_one_ref[...]
    for d in range(3):
        first_sum = first_sum + position[d] * w_pos[d : d + 1]
    act_one = jnp.tanh(first_sum)
    slope_one = 1.0 - act_one * act_one
    curve_one = -2.0 * act_one * slope_one
    pos_square = (
        w_pos[0:1] * w_pos[0:1] + w_pos[1:2] * w_pos[1:2] + w_pos[2:3] * w_pos[2:3]
    )

    def keep(high_ref, low_ref, k, value):
        high, low = halves(value)
        high_ref[k * 128 : (k + 1) * 128] = high
        low_ref[k * 128 : (k + 1) * 128] = low

    keep(act_high, act_low, 0, act_one)
    for d in range(3):
        keep(act_high, act_low, 1 + d, slope_one * w_pos[d : d + 1])
    keep(act_high, act_low, 4, curve_one * pos_square)
    w_mid = halves(w_mid_ref[...])

    def mixed(k):
        rows = slice(k * 128, (k + 1) * 128)
        return product((act_high[rows], act_low[rows]), w_mid, NN)

    act_two = jnp.tanh(mixed(0) + bias_two_ref[...])
    slope_two = 1.0 - act_two * act_two
    curve_two = -2.0 * act_two * slope_two
    mixed_tangent = [mixed(1), mixed(2), mixed(3)]
    mixed_second = mixed(4)
    tangent_square = (
        mixed_tangent[0] * mixed_tangent[0]
        + mixed_tangent[1] * mixed_tangent[1]
        + mixed_tangent[2] * mixed_tangent[2]
    )
    tangent_two = [slope_two * mixed_tangent[d] for d in range(3)]
    second_two = slope_two * mixed_second + curve_two * tangent_square
    w_out = w_out_ref[...]
    w_out_parts = halves(w_out)
    act_two_parts = halves(act_two)
    tangent_parts = [halves(tangent_two[d]) for d in range(3)]
    second_parts = halves(second_two)
    value = product(w_out_parts, act_two_parts, NT) + bias_out_ref[...]
    jets = [product(w_out_parts, tangent_parts[d], NT) for d in range(3)]
    laplace = product(w_out_parts, second_parts, NT)
    prediction_ref[...] = value

    vel = [value[2 + d : 3 + d] for d in range(3)]
    jet = [[jets[d][u : u + 1] for u in range(5)] for d in range(3)]
    continuity = jet[0][2] + jet[1][3] + jet[2][4]
    momentum = []
    for j in range(3):
        term = vel[0] * jet[0][2 + j] + vel[1] * jet[1][2 + j] + vel[2] * jet[2][2 + j]
        term = term + jet[j][1] - VISCOSITY * laplace[2 + j : 3 + j]
        momentum.append(term - value[0:1] if j == 2 else term)
    energy = vel[0] * jet[0][0] + vel[1] * jet[1][0] + vel[2] * jet[2][0]
    energy = energy - DIFFUSIVITY * laplace[0:1]
    miss = value - target_ref[...]
    physics = continuity * continuity + energy * energy
    for j in range(3):
        physics = physics + momentum[j] * momentum[j]
    loss_row = jnp.sum(miss * miss, axis=0, keepdims=True) + RESIDUAL_WEIGHT * physics
    scale = 1.0 / query_total
    loss_row = loss_row * scale
    weight = 2.0 * RESIDUAL_WEIGHT * scale
    cont = continuity * weight
    mom = [momentum[j] * weight for j in range(3)]
    ener = energy * weight
    extra = [-mom[2], jnp.zeros_like(ener)]
    for d in range(3):
        extra.append(
            mom[0] * jet[d][2] + mom[1] * jet[d][3] + mom[2] * jet[d][4] + ener * jet[d][0]
        )
    d_value = (2.0 * scale) * miss + jnp.concatenate(extra, axis=0)
    d_jets = []
    for d in range(3):
        rows = [ener * vel[d], mom[d]]
        for j in range(3):
            rows.append(mom[j] * vel[d] + cont if j == d else mom[j] * vel[d])
        d_jets.append(jnp.concatenate(rows, axis=0))
    d_laplace = jnp.concatenate(
        [-DIFFUSIVITY * ener, jnp.zeros_like(ener)] + [-VISCOSITY * mom[j] for j in range(3)], axis=0
    )
    d_all = [d_value] + d_jets + [d_laplace]
    d_parts = [halves(part) for part in d_all]
    grad_out = product(d_parts[0], act_two_parts, NN)
    for d in range(3):
        grad_out = grad_out + product(d_parts[1 + d], tangent_parts[d], NN)
    grad_out = grad_out + product(d_parts[4], second_parts, NN)

    d_act = product(d_parts[0], w_out_parts, TN)
    d_tangent = [product(d_parts[1 + d], w_out_parts, TN) for d in range(3)]
    d_second = product(d_parts[4], w_out_parts, TN)
    d_slope = d_second * mixed_second
    for d in range(3):
        d_slope = d_slope + d_tangent[d] * mixed_tangent[d]
        keep(
            cot_high, cot_low, 1 + d,
            slope_two * d_tangent[d] + (2.0 * curve_two) * mixed_tangent[d] * d_second,
        )
    keep(cot_high, cot_low, 4, slope_two * d_second)
    d_curve = d_second * tangent_square
    d_slope = d_slope - 2.0 * act_two * d_curve
    d_sum_two = slope_two * (d_act - 2.0 * slope_two * d_curve - 2.0 * act_two * d_slope)
    keep(cot_high, cot_low, 0, d_sum_two)
    grad_bias_two = jnp.sum(d_sum_two, axis=0, keepdims=True)

    def pair_copy(first, count, slot):
        rows = pl.ds(pl.multiple_of(other * 128, 128), 128)
        return pltpu.make_async_remote_copy(
            src_ref=grads.at[pl.ds(first, count), rows],
            dst_ref=pair_buf.at[pl.ds(first, count)],
            send_sem=pair_send.at[slot],
            recv_sem=pair_recv.at[slot],
            device_id=at_tile(chip, other),
            device_id_type=MESH,
        )

    pair_copies = []
    for p in range(8):
        r, c = (p // 4) * 256, (p % 4) * 128
        grads[p] = product(
            (act_high[:, r : r + 256], act_low[:, r : r + 256]),
            (cot_high[:, c : c + 128], cot_low[:, c : c + 128]),
            TN,
        )
        copy = pair_copy(p, 1, p)
        copy.start()
        pair_copies.append(copy)

    mine = pl.ds(pl.multiple_of(core * 128, 128), 128)

    def plane_copies(first, count, group):
        copies = []
        for step, chip_index in enumerate(chips):
            rows = pl.ds(pl.multiple_of(core * 128 + chip_index * rows_xy, 8), rows_xy)
            copies.append(
                pltpu.make_async_remote_copy(
                    src_ref=grads.at[pl.ds(first, count), rows],
                    dst_ref=plane_buf.at[chip, pl.ds(first, count)],
                    send_sem=plane_send.at[group, step],
                    recv_sem=plane_recv.at[group, chip],
                    device_id=at_tile(chip_index, core),
                    device_id_type=MESH,
                )
            )
        return copies

    for p in range(8):
        pair_copies[p].wait()
        grads[p, mine] = grads[p, mine] + pair_buf[p]
    first_group = plane_copies(0, 8, 0)
    for copy in first_group:
        copy.start()

    def back(k):
        rows = slice(k * 128, (k + 1) * 128)
        return product((cot_high[rows], cot_low[rows]), w_mid, NT)

    d_act_one = back(0)
    d_slope_one = jnp.zeros_like(slope_one)
    second_back = back(4)
    second_sum = 2.0 * jnp.sum(second_back * curve_one, axis=0, keepdims=True)
    grad_pos = []
    for d in range(3):
        tangent_back = back(1 + d)
        d_slope_one = d_slope_one + tangent_back * w_pos[d : d + 1]
        grad_pos.append(
            jnp.sum(tangent_back * slope_one, axis=0, keepdims=True)
            + w_pos[d : d + 1] * second_sum
        )
    d_curve_one = second_back * pos_square
    d_slope_one = d_slope_one - 2.0 * act_one * d_curve_one
    d_sum_one = slope_one * (
        d_act_one - 2.0 * slope_one * d_curve_one - 2.0 * act_one * d_slope_one
    )
    for d in range(3):
        grad_pos[d] = grad_pos[d] + jnp.sum(
            d_sum_one * position[d], axis=0, keepdims=True
        )
    grad_bias_one = jnp.sum(d_sum_one, axis=0, keepdims=True)
    sum_high, sum_low = halves(d_sum_one)
    grad_latent = lax.dot_general(
        latent_rows, sum_high, (TN, ((), ())), preferred_element_type=f32
    ) + lax.dot_general(latent_rows, sum_low, (TN, ((), ())), preferred_element_type=f32)
    small = jnp.concatenate(
        grad_pos + [grad_bias_one, grad_bias_two, jnp.zeros((3, 512), f32), grad_out, jnp.zeros((3, 512), f32)],
        axis=0,
    )
    grads[9] = jnp.zeros((256, 128), f32)
    for j in range(4):
        grads[8, j * 64 : (j + 1) * 64] = grad_latent[:, j * 128 : (j + 1) * 128]
        grads[9, j * 64 : j * 64 + 16] = small[:, j * 128 : (j + 1) * 128]
    grads[9, 16:24] = jnp.concatenate([d_value, loss_row, jnp.zeros((2, 128), f32)], axis=0)
    last_pair = pair_copy(8, 2, 8)
    last_pair.start()
    last_pair.wait()
    for p in (8, 9):
        grads[p, mine] = grads[p, mine] + pair_buf[p]
    second_group = plane_copies(8, 2, 1)
    for copy in second_group:
        copy.start()

    for group, copies in ((0, first_group), (1, second_group)):
        for step, chip_index in enumerate(chips):
            copies[step].wait_send()
            pltpu.make_async_remote_copy(
                src_ref=plane_buf.at[chip_index, pl.ds(0 if group == 0 else 8, 8 if group == 0 else 2)],
                dst_ref=plane_buf.at[chip_index, pl.ds(0 if group == 0 else 8, 8 if group == 0 else 2)],
                send_sem=plane_send.at[group, step],
                recv_sem=plane_recv.at[group, chip_index],
                device_id=at_tile(chip_index, core),
                device_id_type=MESH,
            ).wait_recv()
    own = pl.ds(pl.multiple_of(core * 128 + chip * rows_xy, 8), rows_xy)
    total = grads[:, own]
    for chip_index in chips:
        total = total + plane_buf[chip_index]

    for k in range(n_z):
        for p in range(PLANES):
            z_send[k, p * rows_z : (p + 1) * rows_z] = total[p, k * rows_z : (k + 1) * rows_z]

    def exchange(source, target, send_sems, recv_sems):
        copies = []
        for step, z_index in enumerate(depths):
            copy = pltpu.make_async_remote_copy(
                src_ref=source(z_index),
                dst_ref=target.at[z],
                send_sem=send_sems.at[step],
                recv_sem=recv_sems.at[z],
                device_id=at_z(z_index),
                device_id_type=MESH,
            )
            copy.start()
            copies.append(copy)
        for step, z_index in enumerate(depths):
            copies[step].wait_send()
            pltpu.make_async_remote_copy(
                src_ref=target.at[z_index],
                dst_ref=target.at[z_index],
                send_sem=send_sems.at[step],
                recv_sem=recv_sems.at[z_index],
                device_id=at_z(z_index),
                device_id_type=MESH,
            ).wait_recv()

    exchange(lambda z_index: z_send.at[z_index], z_buf, zs_send, zs_recv)
    reduced = z_send[z]
    for z_index in depths:
        reduced = reduced + z_buf[z_index]
    z_all[z] = reduced
    exchange(lambda z_index: z_all.at[z], z_all, zg_send, zg_recv)

    for k in range(n_z):
        for p in range(PLANES):
            piece[p, k * rows_z : (k + 1) * rows_z] = z_all[k, p * rows_z : (p + 1) * rows_z]
    packed_ref[:, own] = piece[...]
    gathered = []
    for step, chip_index in enumerate(chips):
        copy = pltpu.make_async_remote_copy(
            src_ref=piece,
            dst_ref=packed_ref.at[:, own],
            send_sem=pg_send.at[step],
            recv_sem=pg_recv.at[chip],
            device_id=at_tile(chip_index, core),
            device_id_type=MESH,
        )
        copy.start()
        gathered.append(copy)

    def cross(chip_index, slot, core_index):
        rows = pl.ds(pl.multiple_of(core_index * 128 + chip_index * rows_xy, 8), rows_xy)
        return pltpu.make_async_remote_copy(
            src_ref=packed_ref.at[:, rows],
            dst_ref=packed_ref.at[:, rows],
            send_sem=cg_send.at[slot],
            recv_sem=cg_recv.at[slot],
            device_id=at_tile(chip, other),
            device_id_type=MESH,
        )

    crossed = [cross(chip, 0, core)]
    crossed[0].start()
    for step, chip_index in enumerate(chips):
        rows = pl.ds(pl.multiple_of(core * 128 + chip_index * rows_xy, 8), rows_xy)
        pltpu.make_async_remote_copy(
            src_ref=piece,
            dst_ref=packed_ref.at[:, rows],
            send_sem=pg_send.at[step],
            recv_sem=pg_recv.at[chip_index],
            device_id=at_tile(chip_index, core),
            device_id_type=MESH,
        ).wait_recv()
        copy = cross(chip_index, step + 1, core)
        copy.start()
        crossed.append(copy)
    for copy in gathered:
        copy.wait_send()
    for slot in range(n_xy):
        crossed[slot].wait_send()
        chip_index = chip if slot == 0 else chips[slot - 1]
        cross(chip_index, slot, other).wait_recv()


def whole_step(
    sizes, fields, weight, conv_bias, owner, cell, frac, target, w_latent, w_pos, bias_one, w_mid, bias_two, w_out, bias_out
):
    n_z, n_tile, _ = sizes
    n_xy = n_tile // 2
    rows_xy = 128 // n_xy
    rows_z = rows_xy // n_z
    hidden = w_mid.shape[0]
    DMA = pltpu.SemaphoreType.DMA
    return pl.pallas_call(
        functools.partial(step_kernel, sizes),
        out_shape=(
            jax.ShapeDtypeStruct((5, 128), f32),
            jax.ShapeDtypeStruct((PLANES, 256, 128), f32),
        ),
        in_specs=[pl.BlockSpec(memory_space=pltpu.VMEM)] * 14,
        out_specs=[pl.BlockSpec(memory_space=pltpu.VMEM)] * 2,
        scratch_shapes=[
            pltpu.VMEM((PLANES, 256, 128), f32),
            pltpu.VMEM((PLANES, 128, 128), f32),
            pltpu.VMEM((n_xy, PLANES, rows_xy, 128), f32),
            pltpu.VMEM((n_z, PLANES * rows_z, 128), f32),
            pltpu.VMEM((n_z, PLANES * rows_z, 128), f32),
            pltpu.VMEM((n_z, PLANES * rows_z, 128), f32),
            pltpu.VMEM((PLANES, rows_xy, 128), f32),
            pltpu.VMEM((640, hidden), bf16),
            pltpu.VMEM((640, hidden), bf16),
            pltpu.VMEM((640, hidden), bf16),
            pltpu.VMEM((640, hidden), bf16),
            DMA((9,)), DMA((9,)),
            DMA((2, n_xy)), DMA((2, n_xy)),
            DMA((n_z,)), DMA((n_z,)),
            DMA((n_z,)), DMA((n_z,)),
            DMA((n_xy,)), DMA((n_xy,)),
            DMA((n_xy,)), DMA((n_xy,)),
            pltpu.VMEM((5, 128, 512), bf16),
            pltpu.VMEM((768, 384), bf16),
            pltpu.VMEM((2560, 128), bf16),
            pltpu.VMEM((2, 256, 2560), bf16),
            pltpu.VMEM((256, 128), f32),
            pltpu.VMEM((256, 128), f32),
            pltpu.VMEM((256, 128), f32),
            pltpu.VMEM((256, 128), f32),
            DMA((5,)), DMA((5,)),
            DMA((n_tile,)), DMA((n_tile,)),
            DMA((n_tile,)), DMA((n_tile,)),
        ],
        compiler_params=pltpu.CompilerParams(
            collective_id=0, has_side_effects=True, vmem_limit_bytes=48 << 20
        ),
        name="step",
    )(
        fields, weight, conv_bias.reshape(1, -1), owner, cell, frac, target, w_latent, w_pos, bias_one.reshape(1, -1), w_mid,
        bias_two.reshape(1, -1), w_out, bias_out.reshape(-1, 1),
    )


def unpack_kernel(
    prediction_ref, packed_ref, value_ref, latent_ref, pos_ref, one_ref, mid_ref, two_ref, out_ref, bias_ref, loss_ref
):
    value_ref[...] = prediction_ref[...]
    for p in range(8):
        r, c = (p // 4) * 256, (p % 4) * 128
        mid_ref[r : r + 256, c : c + 128] = packed_ref[p]
    for j in range(4):
        columns = slice(j * 128, (j + 1) * 128)
        latent_ref[:, columns] = packed_ref[8, j * 64 : (j + 1) * 64]
        small = packed_ref[9, j * 64 : j * 64 + 16]
        pos_ref[:, columns] = small[0:3]
        one_ref[:, columns] = small[3:4]
        two_ref[:, columns] = small[4:5]
        out_ref[:, columns] = small[8:13]
    sums = jnp.sum(packed_ref[9, 16:24], axis=1, keepdims=True)
    loss_ref[...] = sums[5:6]
    eye = lax.broadcasted_iota(jnp.int32, (8, 128), 0) == lax.broadcasted_iota(jnp.int32, (8, 128), 1)
    bias_ref[...] = jnp.sum(jnp.where(eye, jnp.broadcast_to(sums, (8, 128)), 0.0), axis=0, keepdims=True)[:, :5]


def unpacked(prediction, packed):
    shapes = ((5, 128), (64, 512), (3, 512), (1, 512), (512, 512), (1, 512), (5, 512), (1, 5), (1, 1))
    value, latent, pos, one, mid, two, out, bias, loss = pl.pallas_call(
        unpack_kernel,
        out_shape=tuple(jax.ShapeDtypeStruct(shape, f32) for shape in shapes),
        in_specs=[pl.BlockSpec(memory_space=pltpu.VMEM)] * 2,
        out_specs=[pl.BlockSpec(memory_space=pltpu.VMEM)] * 9,
        name="unpack",
    )(prediction, packed)
    return (value[None], latent, pos, one[0], mid, two[0], out, bias[0], loss[0, 0])


def body(
    fields,
    convolution_weight,
    convolution_bias,
    query_owner,
    query_cell,
    query_frac,
    target,
    w_latent,
    w_pos,
    bias_one,
    w_mid,
    bias_two,
    w_out,
    bias_out,
):
    tile_count = lax.axis_size("tile")
    replica_count = lax.axis_size("replica")
    channels, planes, rows_y, rows_z = fields.shape[1:]
    turned = jnp.transpose(jnp.roll(fields[0], 1, axis=2), (1, 3, 2, 0))
    turned = turned.reshape(planes, rows_z, rows_y * channels)
    query_count = query_cell.shape[1]
    query_total = float(query_count * tile_count * replica_count)
    prediction, packed = whole_step(
        (replica_count, tile_count, query_total),
        turned,
        convolution_weight,
        convolution_bias,
        query_owner.reshape(1, query_count),
        query_cell,
        query_frac[0],
        target[0],
        w_latent,
        w_pos,
        bias_one,
        w_mid,
        bias_two,
        w_out,
        bias_out,
    )
    return unpacked(prediction, packed)


def solution(mesh):
    return jax.shard_map(
        body,
        mesh=mesh,
        in_specs=(
            P("replica", None, "tile", None, None),
            P(),
            P(),
            P("replica", "tile", None),
            P("replica", "tile"),
            P("replica", None, "tile"),
            P("replica", None, "tile"),
            P(),
            P(),
            P(),
            P(),
            P(),
            P(),
            P(),
        ),
        out_specs=(P("replica", None, "tile"), P(), P(), P(), P(), P(), P(), P(), P()),
        check_vma=False,
    )
```

profile of v0, /device:TPU:1, one launch (start us, length us, event | category | flops | bytes accessed | tf_op | source)
XLA Modules:
  0.0 81.4 jit_solution(13931892320910943029)
XLA Ops:
  0.6 0.7 copy.37
  1.3 0.7 copy.36
  2.0 0.7 copy.28.bias_out_ref
  2.7 1.2 %copy.35 = bf16[1,64,4,8,128]{4,1,3,2,0:T(8,128)(2,1)S(1)} copy(bf16[1,64,4,8,128]{4,3,2,1,0:T(8,128)(2,1)} %param.14) | data formatting | bytes 1048576 | tf_op args[0]
  4.0 0.0 copy-start.1
  4.0 0.0 copy-start.2
  4.0 0.0 copy-start.3
  4.0 0.0 copy-start.4
  4.1 0.0 copy-start.5
  4.1 0.0 copy-start.7
  4.1 0.0 copy-start.8
  4.1 0.0 copy-start.9
  4.1 0.0 copy-start.10
  4.1 0.0 copy-start.11
  4.2 0.2 copy.27.fields_ref
  4.5 0.8 copy-done.1
  5.2 0.0 copy-done.2
  5.3 0.0 copy-done.3
  5.3 0.0 copy-done.4
  5.3 0.0 copy-done.5
  5.3 0.0 copy-done.7
  5.3 0.0 copy-done.8
  5.3 0.0 copy-done.9
  5.3 0.0 copy-done.10
  5.3 0.0 copy-done.11
  5.3 70.7 %step.1 = (f32[5,128]{1,0:T(8,128)S(1)}, f32[10,256,128]{2,1,0:T(8,128)S(1)}) custom-call(bf16[4,128,512]{2,1,0:T(8,128)(2,1)S(1)} %copy.27.fields_ref, bf16[64,1728]{1,0:T(8,128)(2,1)S(1)} %copy-done.2, f32[1,64]{1,0:T(1,128)S(1)} %bitcast.26, s32[1,128]{1,0:T(1,128)S(1)} %bitcast.27, s32[1,128]{1,0:T(1,128)S(1)} %copy-done.11, f32[3,128]{1,0:T(4,128)S(1)} %bitcast.23, ...), custom_call_target="tpu_custom_call" | custom-call | tf_op jit(solution)/shard_map/step/pallas_call | solution.py:592
  76.0 0.0 copy-start
  76.1 1.1 %copy-done = f32[10,256,128]{2,1,0:T(8,128)} copy-done((f32[10,256,128]{2,1,0:T(8,128)}, f32[10,256,128]{2,1,0:T(8,128)S(1)}, u32[]{:S(2)}) %copy-start) | copy-done | bytes 1310744
  77.1 0.0 copy-start.6
  77.1 0.6 copy-done.6
  77.7 2.4 %unpack.1 = (f32[5,128]{1,0:T(8,128)}, f32[64,512]{1,0:T(8,128)}, f32[3,512]{1,0:T(4,128)}, f32[1,512]{1,0:T(1,128)}, f32[512,512]{1,0:T(8,128)}, /*index=5*/f32...) custom-call(f32[5,128]{1,0:T(8,128)} %copy-done.6, f32[10,256,128]{2,1,0:T(8,128)} %copy-done), custom_call_target="tpu_custom_call" | custom-call | tf_op jit(solution)/shard_map/unpack/pallas_call | solution.py:663
  80.2 1.3 %copy.29 = f32[1,5,128]{2,0,1:T(1,128)} copy(f32[1,5,128]{2,1,0:T(8,128)} %bitcast.31) | data formatting | bytes 5120
  (3 shorter events, 0.1 us)
Async XLA Ops:
  4.0 1.2 %copy-start.1 = (f32[512,512]{1,0:T(8,128)S(1)}, f32[512,512]{1,0:T(8,128)}, u32[]{:S(2)}) copy-start(f32[512,512]{1,0:T(8,128)} %w_mid_ref.1) | copy-start | bytes 3145732
  4.0 1.2 %copy-start.2 = (bf16[64,1728]{1,0:T(8,128)(2,1)S(1)}, bf16[64,1728]{1,0:T(8,128)(2,1)}, u32[]{:S(2)}) copy-start(bf16[64,1728]{1,0:T(8,128)(2,1)} %weight_ref.1) | copy-start | bytes 663556
  4.0 1.3 %copy-start.3 = (f32[64,512]{1,0:T(8,128)S(1)}, f32[64,512]{1,0:T(8,128)}, u32[]{:S(2)}) copy-start(f32[64,512]{1,0:T(8,128)} %w_latent_ref.1) | copy-start | bytes 393220
  4.0 1.3 %copy-start.4 = (f32[5,512]{1,0:T(8,128)S(1)}, f32[5,512]{1,0:T(8,128)}, u32[]{:S(2)}) copy-start(f32[5,512]{1,0:T(8,128)} %w_out_ref.1) | copy-start | bytes 30724
  4.1 1.2 %copy-start.5 = (f32[3,512]{1,0:T(4,128)S(1)}, f32[3,512]{1,0:T(4,128)}, u32[]{:S(2)}) copy-start(f32[3,512]{1,0:T(4,128)} %w_pos_ref.1) | copy-start | bytes 18436
  4.1 1.2 %copy-start.7 = (f32[512]{0:T(512)S(1)}, f32[512]{0:T(512)}, u32[]{:S(2)}) copy-start(f32[512]{0:T(512)} %param.23) | copy-start | bytes 6148
  4.1 1.2 %copy-start.8 = (f32[512]{0:T(512)S(1)}, f32[512]{0:T(512)}, u32[]{:S(2)}) copy-start(f32[512]{0:T(512)} %param.25) | copy-start | bytes 6148
  4.1 1.2 %copy-start.9 = (f32[64]{0:T(128)S(1)}, f32[64]{0:T(128)}, u32[]{:S(2)}) copy-start(f32[64]{0:T(128)} %param.16) | copy-start | bytes 772
  4.1 1.2 %copy-start.10 = (s32[1,128,1]{1,2,0:T(1,128)S(1)}, s32[1,128,1]{1,2,0:T(1,128)}, u32[]{:S(2)}) copy-start(s32[1,128,1]{1,2,0:T(1,128)} %param.17) | copy-start | bytes 1540
  4.1 1.2 %copy-start.11 = (s32[1,128]{1,0:T(1,128)S(1)}, s32[1,128]{1,0:T(1,128)}, u32[]{:S(2)}) copy-start(s32[1,128]{1,0:T(1,128)} %cell_ref.1) | copy-start | bytes 1540
  76.0 1.1 %copy-start = (f32[10,256,128]{2,1,0:T(8,128)}, f32[10,256,128]{2,1,0:T(8,128)S(1)}, u32[]{:S(2)}) copy-start(f32[10,256,128]{2,1,0:T(8,128)S(1)} %get-tuple-element.21.packed_ref) | copy-start | bytes 3932164
  77.1 0.6 copy-start.6
where the time goes:
time: 81.7 us; the launch traced here: 81.4 us
  Pallas kernels  73.1 us (89%)
  local copies, waits for them, and re-layouts  7.44 us (9%)
    pallas_call x1, Pallas kernels, whole_step(): pl.pallas_call(functools.partial(step_kernel, sizes), out_shape=(jax.Shap...  70.7 us
    unnamed x28, local copies, waits for them, and re-layouts  6.44 us
    pallas_call x1, Pallas kernels, unpacked(): pl.pallas_call(unpack_kernel, out_shape=tuple((jax.ShapeDtypeStruct(shape...  2.44 us

commit v1 on v0

--- a/solution.py
+++ b/solution.py
@@ -97,7 +97,7 @@
         lax.broadcasted_iota(jnp.int32, (128, 256), 1) == jnp.broadcast_to(key_column, (128, 256))
     ).astype(f32).astype(bf16)
     cell = cell_ref[...]
-    fraction = frac_ref[...]
+    fraction = jnp.concatenate([frac_ref[d] for d in range(3)], axis=0)
     listed = [(cell // 64).astype(f32), (cell % 64).astype(f32)]
     for d in range(3):
         rest = fraction[d : d + 1]
@@ -111,35 +111,31 @@
     )
     wanted[...] = asking
 
-    def exchange(source, target, send_sems, recv_sems):
+    def exchange(source, target, send_sem, recv_sem):
         mine = pl.ds(pl.multiple_of(tile * slots, 8), slots)
-        copies = []
-        for step, index in enumerate(others):
+        for index in others:
             theirs = pl.ds(pl.multiple_of(index * slots, 8), slots)
             copy = pltpu.make_async_remote_copy(
                 src_ref=source.at[theirs],
                 dst_ref=target.at[mine],
-                send_sem=send_sems.at[step],
-                recv_sem=recv_sems.at[tile],
+                send_sem=send_sem,
+                recv_sem=recv_sem,
                 device_id=at_tile(index),
                 device_id_type=MESH,
             )
             copy.start()
-            copies.append(copy)
         target[mine] = source[mine]
 
         def finish():
-            for step, index in enumerate(others):
-                theirs = pl.ds(pl.multiple_of(index * slots, 8), slots)
-                copies[step].wait_send()
-                pltpu.make_async_remote_copy(
-                    src_ref=target.at[theirs],
-                    dst_ref=target.at[theirs],
-                    send_sem=send_sems.at[step],
-                    recv_sem=recv_sems.at[index],
-                    device_id=at_tile(index),
-                    device_id_type=MESH,
-                ).wait_recv()
+            every = pl.ds(0, (n_tile - 1) * slots)
+            pltpu.make_async_remote_copy(
+                src_ref=source.at[every],
+                dst_ref=target.at[every],
+                send_sem=send_sem,
+                recv_sem=recv_sem,
+                device_id=at_tile(above),
+                device_id_type=MESH,
+            ).wait()
 
         return finish
 
@@ -240,6 +236,7 @@
     act_high, act_low, cot_high, cot_low,
     pair_send, pair_recv, plane_send, plane_recv, zs_send, zs_recv, zg_send, zg_recv,
     pg_send, pg_recv, cg_send, cg_recv,
+    w_mid_buf, w_mid_sem,
     *encode_scratch,
 ):
     n_z, n_tile, query_total = sizes
@@ -260,6 +257,8 @@
 
     chips = [lax.rem(chip + step, n_xy) for step in range(1, n_xy)]
     depths = [lax.rem(z + step, n_z) for step in range(1, n_z)]
+    w_mid_copy = pltpu.make_async_copy(w_mid_ref, w_mid_buf, w_mid_sem)
+    w_mid_copy.start()
     barrier = pltpu.get_barrier_semaphore()
     for step in range(1, n_tile):
         pl.semaphore_signal(
@@ -294,7 +293,8 @@
     for d in range(3):
         keep(act_high, act_low, 1 + d, slope_one * w_pos[d : d + 1])
     keep(act_high, act_low, 4, curve_one * pos_square)
-    w_mid = halves(w_mid_ref[...])
+    w_mid_copy.wait()
+    w_mid = halves(w_mid_buf[...])
 
     def mixed(k):
         rows = slice(k * 128, (k + 1) * 128)
@@ -317,10 +317,21 @@
     act_two_parts = halves(act_two)
     tangent_parts = [halves(tangent_two[d]) for d in range(3)]
     second_parts = halves(second_two)
-    value = product(w_out_parts, act_two_parts, NT) + bias_out_ref[...]
+    square = (5, 5)
+    bias_out = jnp.sum(
+        jnp.where(
+            lax.broadcasted_iota(jnp.int32, square, 0) == lax.broadcasted_iota(jnp.int32, square, 1),
+            jnp.broadcast_to(bias_out_ref[...], square),
+            0.0,
+        ),
+        axis=1,
+        keepdims=True,
+    )
+    value = product(w_out_parts, act_two_parts, NT) + bias_out
     jets = [product(w_out_parts, tangent_parts[d], NT) for d in range(3)]
     laplace = product(w_out_parts, second_parts, NT)
-    prediction_ref[...] = value
+    for u in range(5):
+        prediction_ref[u] = value[u : u + 1]
 
     vel = [value[2 + d : 3 + d] for d in range(3)]
     jet = [[jets[d][u : u + 1] for u in range(5)] for d in range(3)]
@@ -332,7 +343,7 @@
         momentum.append(term - value[0:1] if j == 2 else term)
     energy = vel[0] * jet[0][0] + vel[1] * jet[1][0] + vel[2] * jet[2][0]
     energy = energy - DIFFUSIVITY * laplace[0:1]
-    miss = value - target_ref[...]
+    miss = value - jnp.concatenate([target_ref[u] for u in range(5)], axis=0)
     physics = continuity * continuity + energy * energy
     for j in range(3):
         physics = physics + momentum[j] * momentum[j]
@@ -409,14 +420,14 @@
 
     def plane_copies(first, count, group):
         copies = []
-        for step, chip_index in enumerate(chips):
+        for chip_index in chips:
             rows = pl.ds(pl.multiple_of(core * 128 + chip_index * rows_xy, 8), rows_xy)
             copies.append(
                 pltpu.make_async_remote_copy(
                     src_ref=grads.at[pl.ds(first, count), rows],
                     dst_ref=plane_buf.at[chip, pl.ds(first, count)],
-                    send_sem=plane_send.at[group, step],
-                    recv_sem=plane_recv.at[group, chip],
+                    send_sem=plane_send.at[group],
+                    recv_sem=plane_recv.at[group],
                     device_id=at_tile(chip_index, core),
                     device_id_type=MESH,
                 )
@@ -478,17 +489,16 @@
     for copy in second_group:
         copy.start()
 
-    for group, copies in ((0, first_group), (1, second_group)):
-        for step, chip_index in enumerate(chips):
-            copies[step].wait_send()
-            pltpu.make_async_remote_copy(
-                src_ref=plane_buf.at[chip_index, pl.ds(0 if group == 0 else 8, 8 if group == 0 else 2)],
-                dst_ref=plane_buf.at[chip_index, pl.ds(0 if group == 0 else 8, 8 if group == 0 else 2)],
-                send_sem=plane_send.at[group, step],
-                recv_sem=plane_recv.at[group, chip_index],
-                device_id=at_tile(chip_index, core),
-                device_id_type=MESH,
-            ).wait_recv()
+    for group, first, count in ((0, 0, 8), (1, 8, 2)):
+        block = plane_buf.at[pl.ds(0, n_xy - 1), pl.ds(first, count)]
+        pltpu.make_async_remote_copy(
+            src_ref=block,
+            dst_ref=block,
+            send_sem=plane_send.at[group],
+            recv_sem=plane_recv.at[group],
+            device_id=at_tile(chip, other),
+            device_id_type=MESH,
+        ).wait()
     own = pl.ds(pl.multiple_of(core * 128 + chip * rows_xy, 8), rows_xy)
     total = grads[:, own]
     for chip_index in chips:
@@ -498,29 +508,25 @@
         for p in range(PLANES):
             z_send[k, p * rows_z : (p + 1) * rows_z] = total[p, k * rows_z : (k + 1) * rows_z]
 
-    def exchange(source, target, send_sems, recv_sems):
-        copies = []
-        for step, z_index in enumerate(depths):
-            copy = pltpu.make_async_remote_copy(
+    def exchange(source, target, send_sem, recv_sem):
+        for z_index in depths:
+            pltpu.make_async_remote_copy(
                 src_ref=source(z_index),
                 dst_ref=target.at[z],
-                send_sem=send_sems.at[step],
-                recv_sem=recv_sems.at[z],
+                send_sem=send_sem,
+                recv_sem=recv_sem,
                 device_id=at_z(z_index),
                 device_id_type=MESH,
-            )
-            copy.start()
-            copies.append(copy)
-        for step, z_index in enumerate(depths):
-            copies[step].wait_send()
-            pltpu.make_async_remote_copy(
-                src_ref=target.at[z_index],
-                dst_ref=target.at[z_index],
-                send_sem=send_sems.at[step],
-                recv_sem=recv_sems.at[z_index],
-                device_id=at_z(z_index),
-                device_id_type=MESH,
-            ).wait_recv()
+            ).start()
+        block = target.at[pl.ds(0, n_z - 1)]
+        pltpu.make_async_remote_copy(
+            src_ref=block,
+            dst_ref=block,
+            send_sem=send_sem,
+            recv_sem=recv_sem,
+            device_id=at_tile(chip, other),
+            device_id_type=MESH,
+        ).wait()
 
     exchange(lambda z_index: z_send.at[z_index], z_buf, zs_send, zs_recv)
     reduced = z_send[z]
@@ -533,51 +539,58 @@
         for p in range(PLANES):
             piece[p, k * rows_z : (k + 1) * rows_z] = z_all[k, p * rows_z : (p + 1) * rows_z]
     packed_ref[:, own] = piece[...]
-    gathered = []
-    for step, chip_index in enumerate(chips):
+    for chip_index in chips:
         copy = pltpu.make_async_remote_copy(
             src_ref=piece,
             dst_ref=packed_ref.at[:, own],
-            send_sem=pg_send.at[step],
+            send_sem=pg_send,
             recv_sem=pg_recv.at[chip],
             device_id=at_tile(chip_index, core),
             device_id_type=MESH,
         )
         copy.start()
-        gathered.append(copy)
-
-    def cross(chip_index, slot, core_index):
-        rows = pl.ds(pl.multiple_of(core_index * 128 + chip_index * rows_xy, 8), rows_xy)
+
+    def cross(chip_index):
+        rows = pl.ds(pl.multiple_of(core * 128 + chip_index * rows_xy, 8), rows_xy)
         return pltpu.make_async_remote_copy(
             src_ref=packed_ref.at[:, rows],
             dst_ref=packed_ref.at[:, rows],
-            send_sem=cg_send.at[slot],
-            recv_sem=cg_recv.at[slot],
+            send_sem=cg_send,
+            recv_sem=cg_recv,
             device_id=at_tile(chip, other),
             device_id_type=MESH,
         )
 
-    crossed = [cross(chip, 0, core)]
-    crossed[0].start()
-    for step, chip_index in enumerate(chips):
+    cross(chip).start()
+    for chip_index in chips:
         rows = pl.ds(pl.multiple_of(core * 128 + chip_index * rows_xy, 8), rows_xy)
         pltpu.make_async_remote_copy(
             src_ref=piece,
             dst_ref=packed_ref.at[:, rows],
-            send_sem=pg_send.at[step],
+            send_sem=pg_send,
             recv_sem=pg_recv.at[chip_index],
             device_id=at_tile(chip_index, core),
             device_id_type=MESH,
         ).wait_recv()
-        copy = cross(chip_index, step + 1, core)
-        copy.start()
-        crossed.append(copy)
-    for copy in gathered:
-        copy.wait_send()
-    for slot in range(n_xy):
-        crossed[slot].wait_send()
-        chip_index = chip if slot == 0 else chips[slot - 1]
-        cross(chip_index, slot, other).wait_recv()
+        cross(chip_index).start()
+    half = packed_ref.at[:, pl.ds(0, (n_xy - 1) * rows_xy)]
+    pltpu.make_async_remote_copy(
+        src_ref=half,
+        dst_ref=half,
+        send_sem=pg_send,
+        recv_sem=pg_recv.at[chip],
+        device_id=at_tile(chip, other),
+        device_id_type=MESH,
+    ).wait_send()
+    half = packed_ref.at[:, pl.ds(0, 128)]
+    pltpu.make_async_remote_copy(
+        src_ref=half,
+        dst_ref=half,
+        send_sem=cg_send,
+        recv_sem=cg_recv,
+        device_id=at_tile(chip, other),
+        device_id_type=MESH,
+    ).wait()
 
 
 def whole_step(
@@ -592,10 +605,12 @@
     return pl.pallas_call(
         functools.partial(step_kernel, sizes),
         out_shape=(
-            jax.ShapeDtypeStruct((5, 128), f32),
+            jax.ShapeDtypeStruct((5, 1, 128), f32),
             jax.ShapeDtypeStruct((PLANES, 256, 128), f32),
         ),
-        in_specs=[pl.BlockSpec(memory_space=pltpu.VMEM)] * 14,
+        in_specs=[
+            pl.BlockSpec(memory_space=pltpu.HBM if k == 10 else pltpu.VMEM) for k in range(14)
+        ],
         out_specs=[pl.BlockSpec(memory_space=pltpu.VMEM)] * 2,
         scratch_shapes=[
             pltpu.VMEM((PLANES, 256, 128), f32),
@@ -610,11 +625,13 @@
             pltpu.VMEM((640, hidden), bf16),
             pltpu.VMEM((640, hidden), bf16),
             DMA((9,)), DMA((9,)),
-            DMA((2, n_xy)), DMA((2, n_xy)),
-            DMA((n_z,)), DMA((n_z,)),
-            DMA((n_z,)), DMA((n_z,)),
-            DMA((n_xy,)), DMA((n_xy,)),
-            DMA((n_xy,)), DMA((n_xy,)),
+            DMA((2,)), DMA((2,)),
+            DMA(()), DMA(()),
+            DMA(()), DMA(()),
+            DMA(()), DMA((n_xy,)),
+            DMA(()), DMA(()),
+            pltpu.VMEM((hidden, hidden), f32),
+            DMA(()),
             pltpu.VMEM((5, 128, 512), bf16),
             pltpu.VMEM((768, 384), bf16),
             pltpu.VMEM((2560, 128), bf16),
@@ -624,8 +641,8 @@
             pltpu.VMEM((256, 128), f32),
             pltpu.VMEM((256, 128), f32),
             DMA((5,)), DMA((5,)),
-            DMA((n_tile,)), DMA((n_tile,)),
-            DMA((n_tile,)), DMA((n_tile,)),
+            DMA(()), DMA(()),
+            DMA(()), DMA(()),
         ],
         compiler_params=pltpu.CompilerParams(
             collective_id=0, has_side_effects=True, vmem_limit_bytes=48 << 20
@@ -633,17 +650,22 @@
         name="step",
     )(
         fields, weight, conv_bias.reshape(1, -1), owner, cell, frac, target, w_latent, w_pos, bias_one.reshape(1, -1), w_mid,
-        bias_two.reshape(1, -1), w_out, bias_out.reshape(-1, 1),
+        bias_two.reshape(1, -1), w_out, bias_out.reshape(1, -1),
     )
 
 
 def unpack_kernel(
-    prediction_ref, packed_ref, value_ref, latent_ref, pos_ref, one_ref, mid_ref, two_ref, out_ref, bias_ref, loss_ref
+    prediction_ref, packed_ref, value_ref, latent_ref, pos_ref, one_ref, mid_ref, two_ref, out_ref, bias_ref, loss_ref, sem
 ):
-    value_ref[...] = prediction_ref[...]
+    copies = []
     for p in range(8):
         r, c = (p // 4) * 256, (p % 4) * 128
-        mid_ref[r : r + 256, c : c + 128] = packed_ref[p]
+        copies.append(
+            pltpu.make_async_copy(packed_ref.at[p], mid_ref.at[pl.ds(r, 256), pl.ds(c, 128)], sem.at[p])
+        )
+    for copy in copies:
+        copy.start()
+    value_ref[...] = prediction_ref[...]
     for j in range(4):
         columns = slice(j * 128, (j + 1) * 128)
         latent_ref[:, columns] = packed_ref[8, j * 64 : (j + 1) * 64]
@@ -654,20 +676,26 @@
         out_ref[:, columns] = small[8:13]
     sums = jnp.sum(packed_ref[9, 16:24], axis=1, keepdims=True)
     loss_ref[...] = sums[5:6]
-    eye = lax.broadcasted_iota(jnp.int32, (8, 128), 0) == lax.broadcasted_iota(jnp.int32, (8, 128), 1)
-    bias_ref[...] = jnp.sum(jnp.where(eye, jnp.broadcast_to(sums, (8, 128)), 0.0), axis=0, keepdims=True)[:, :5]
+    diagonal = lax.broadcasted_iota(jnp.int32, (8, 128), 0) == lax.broadcasted_iota(jnp.int32, (8, 128), 1)
+    bias_ref[...] = jnp.sum(
+        jnp.where(diagonal, jnp.broadcast_to(sums, (8, 128)), 0.0), axis=0, keepdims=True
+    )[:, :5]
+    for copy in copies:
+        copy.wait()
 
 
 def unpacked(prediction, packed):
-    shapes = ((5, 128), (64, 512), (3, 512), (1, 512), (512, 512), (1, 512), (5, 512), (1, 5), (1, 1))
+    shapes = ((5, 1, 128), (64, 512), (3, 512), (1, 512), (512, 512), (1, 512), (5, 512), (1, 5), (1, 1))
     value, latent, pos, one, mid, two, out, bias, loss = pl.pallas_call(
         unpack_kernel,
         out_shape=tuple(jax.ShapeDtypeStruct(shape, f32) for shape in shapes),
         in_specs=[pl.BlockSpec(memory_space=pltpu.VMEM)] * 2,
-        out_specs=[pl.BlockSpec(memory_space=pltpu.VMEM)] * 9,
+        out_specs=[pl.BlockSpec(memory_space=pl.ANY if k == 4 else pltpu.VMEM) for k in range(9)],
+        scratch_shapes=[pltpu.SemaphoreType.DMA((8,))],
+        compiler_params=pltpu.CompilerParams(vmem_limit_bytes=8 << 20),
         name="unpack",
     )(prediction, packed)
-    return (value[None], latent, pos, one[0], mid, two[0], out, bias[0], loss[0, 0])
+    return (jnp.transpose(value, (1, 0, 2)), latent, pos, one[0], mid, two[0], out, bias[0], loss[0, 0])
 
 
 def body(
@@ -700,8 +728,8 @@
         convolution_bias,
         query_owner.reshape(1, query_count),
         query_cell,
-        query_frac[0],
-        target[0],
+        jnp.transpose(query_frac, (1, 0, 2)),
+        jnp.transpose(target, (1, 0, 2)),
         w_latent,
         w_pos,
         bias_one,

time: 81.7 us -> 73.5 us (0.90)
  local copies, waits for them, and re-layouts: 7.44 us -> 2.39 us
  Pallas kernels: 73.1 us -> 70.1 us
    unnamed x28 -> x27, local copies, waits for them, and re-layouts: 6.44 us -> 2.13 us
    pallas_call x1, Pallas kernels: 70.7 us -> 68.4 us  [whole_step(): pl.pallas_call(functools.partial(step_kernel, sizes), out_shape=(jax.Shap...]
where the time goes in v1:
time: 73.5 us; the launch traced here: 73.3 us
  Pallas kernels  70.1 us (95%)
  local copies, waits for them, and re-layouts  2.39 us (3%)
  between operations  0.84 us (1%)
    pallas_call x1, Pallas kernels, whole_step(): pl.pallas_call(functools.partial(step_kernel, sizes), out_shape=(jax.Shap...  68.4 us
    unnamed x27, local copies, waits for them, and re-layouts  2.13 us
    pallas_call x1, Pallas kernels, unpacked(): pl.pallas_call(unpack_kernel, out_shape=tuple((jax.ShapeDtypeStruct(shape...  1.7 us

profile of v1, /device:TPU:1, one launch (start us, length us, event | category | flops | bytes accessed | tf_op | source)
XLA Modules:
  0.0 73.3 jit_solution(17360483522650667439)
XLA Ops:
  0.6 1.2 %copy.27 = bf16[1,64,4,8,128]{4,1,3,2,0:T(8,128)(2,1)S(1)} copy(bf16[1,64,4,8,128]{4,3,2,1,0:T(8,128)(2,1)} %param.14) | data formatting | bytes 1048576 | tf_op args[0]
  1.9 0.0 copy-start
  1.9 0.0 copy-start.1
  1.9 0.0 copy-start.2
  1.9 0.0 copy-start.3
  2.0 0.0 copy-start.4
  2.0 0.0 copy-start.5
  2.0 0.0 copy-start.6
  2.0 0.0 copy-start.7
  2.0 0.0 copy-start.8
  2.0 0.0 copy-start.9
  2.0 0.0 copy-start.10
  2.0 0.0 copy-start.11
  2.0 0.0 copy-start.12
  2.2 0.2 copy.25.fields_ref
  2.4 0.7 %copy-done = f32[512,512]{1,0:T(8,128)S(1)} copy-done((f32[512,512]{1,0:T(8,128)S(1)}, f32[512,512]{1,0:T(8,128)}, u32[]{:S(2)}) %copy-start) | copy-done | bytes 1048600
  3.1 0.0 copy-done.1
  3.2 0.0 copy-done.2
  3.2 0.0 copy-done.3
  3.2 0.0 copy-done.4
  3.2 0.0 copy-done.5
  3.2 0.0 copy-done.6
  3.2 0.0 copy-done.7
  3.2 0.0 copy-done.8
  3.2 0.0 copy-done.9
  3.2 0.0 copy-done.10
  3.2 0.0 copy-done.11
  3.3 0.0 copy-done.12
  3.3 68.4 %step.1 = (f32[5,1,128]{2,1,0:T(1,128)S(1)}, f32[10,256,128]{2,1,0:T(8,128)S(1)}) custom-call(bf16[4,128,512]{2,1,0:T(8,128)(2,1)S(1)} %copy.25.fields_ref, bf16[64,1728]{1,0:T(8,128)(2,1)S(1)} %copy-done.1, f32[1,64]{1,0:T(1,128)S(1)} %bitcast.22, s32[1,128]{1,0:T(1,128)S(1)} %bitcast.23, s32[1,128]{1,0:T(1,128)S(1)} %copy-done.11, ...), custom_call_target="tpu_custom_call" | custom-call | tf_op jit(solution)/shard_map/step/pallas_call | solution.py:605
  71.6 1.7 %unpack.1 = (f32[5,1,128]{2,1,0:T(1,128)}, f32[64,512]{1,0:T(8,128)}, f32[3,512]{1,0:T(4,128)}, f32[1,512]{1,0:T(1,128)}, f32[512,512]{1,0:T(8,128)}, /*index=5*...) custom-call(f32[5,1,128]{2,1,0:T(1,128)S(1)} %get-tuple-element.20.prediction_ref, ...), custom_call_target="tpu_custom_call" | custom-call | tf_op jit(solution)/shard_map/unpack/pallas_call | solution.py:689
  (3 shorter events, 0.1 us)
Async XLA Ops:
  1.9 1.2 %copy-start = (f32[512,512]{1,0:T(8,128)S(1)}, f32[512,512]{1,0:T(8,128)}, u32[]{:S(2)}) copy-start(f32[512,512]{1,0:T(8,128)} %w_mid_ref.1) | copy-start | bytes 3145732
  1.9 1.2 %copy-start.1 = (bf16[64,1728]{1,0:T(8,128)(2,1)S(1)}, bf16[64,1728]{1,0:T(8,128)(2,1)}, u32[]{:S(2)}) copy-start(bf16[64,1728]{1,0:T(8,128)(2,1)} %weight_ref.1) | copy-start | bytes 663556
  1.9 1.3 %copy-start.2 = (f32[64,512]{1,0:T(8,128)S(1)}, f32[64,512]{1,0:T(8,128)}, u32[]{:S(2)}) copy-start(f32[64,512]{1,0:T(8,128)} %w_latent_ref.1) | copy-start | bytes 393220
  1.9 1.3 %copy-start.3 = (f32[5,512]{1,0:T(8,128)S(1)}, f32[5,512]{1,0:T(8,128)}, u32[]{:S(2)}) copy-start(f32[5,512]{1,0:T(8,128)} %w_out_ref.1) | copy-start | bytes 30724
  2.0 1.2 %copy-start.4 = (f32[3,512]{1,0:T(4,128)S(1)}, f32[3,512]{1,0:T(4,128)}, u32[]{:S(2)}) copy-start(f32[3,512]{1,0:T(4,128)} %w_pos_ref.1) | copy-start | bytes 18436
  2.0 1.2 %copy-start.5 = (f32[1,5,128]{2,0,1:T(1,128)S(1)}, f32[1,5,128]{2,0,1:T(1,128)}, u32[]{:S(2)}) copy-start(f32[1,5,128]{2,0,1:T(1,128)} %param.20) | copy-start | bytes 7684
  2.0 1.2 %copy-start.6 = (f32[512]{0:T(512)S(1)}, f32[512]{0:T(512)}, u32[]{:S(2)}) copy-start(f32[512]{0:T(512)} %param.23) | copy-start | bytes 6148
  2.0 1.2 %copy-start.7 = (f32[512]{0:T(512)S(1)}, f32[512]{0:T(512)}, u32[]{:S(2)}) copy-start(f32[512]{0:T(512)} %param.25) | copy-start | bytes 6148
  2.0 1.2 %copy-start.8 = (f32[1,3,128]{2,0,1:T(1,128)S(1)}, f32[1,3,128]{2,0,1:T(1,128)}, u32[]{:S(2)}) copy-start(f32[1,3,128]{2,0,1:T(1,128)} %param.19) | copy-start | bytes 4612
  2.0 1.2 %copy-start.9 = (f32[64]{0:T(128)S(1)}, f32[64]{0:T(128)}, u32[]{:S(2)}) copy-start(f32[64]{0:T(128)} %param.16) | copy-start | bytes 772
  2.0 1.2 %copy-start.10 = (s32[1,128,1]{1,2,0:T(1,128)S(1)}, s32[1,128,1]{1,2,0:T(1,128)}, u32[]{:S(2)}) copy-start(s32[1,128,1]{1,2,0:T(1,128)} %param.17) | copy-start | bytes 1540
  2.0 1.2 %copy-start.11 = (s32[1,128]{1,0:T(1,128)S(1)}, s32[1,128]{1,0:T(1,128)}, u32[]{:S(2)}) copy-start(s32[1,128]{1,0:T(1,128)} %cell_ref.1) | copy-start | bytes 1540
  2.0 1.2 %copy-start.12 = (f32[5]{0:T(128)S(1)}, f32[5]{0:T(128)}, u32[]{:S(2)}) copy-start(f32[5]{0:T(128)} %param.27) | copy-start | bytes 64

commit v2 on v1

--- a/solution.py
+++ b/solution.py
@@ -42,11 +42,11 @@
 TN = ((0,), (0,))
 
 
-def encode_part(place, refs, scratch):
+def encode_part(place, refs, scratch, prepare):
     z, tile, n_tile = place
     fields_ref, weight_ref, conv_bias_ref, owner_ref, cell_ref, frac_ref = refs
     (
-        halo, taps, latent, corner, asked, wanted, answer, answered,
+        halo, taps, partial, latent, corner, asked, wanted, answer, answered,
         halo_send, halo_recv, ask_send, ask_recv, answer_send, answer_recv,
     ) = scratch
     slots = 256 // n_tile
@@ -73,8 +73,6 @@
         3: halo_copy(1, 3, below),
         4: halo_copy(2, 4, below),
     }
-    for copy in halo_copies.values():
-        copy.start()
 
     lane = lax.broadcasted_iota(jnp.int32, (128, 128), 1)
     row = lax.broadcasted_iota(jnp.int32, (128, 128), 0)
@@ -141,6 +139,9 @@
 
     asked_finish = exchange(wanted, asked, ask_send, ask_recv)
 
+    for copy in halo_copies.values():
+        copy.start()
+
     def position_of(base, d, span):
         return as_column((base.astype(f32) + fraction[d : d + 1]) * (1.0 / span))
 
@@ -166,6 +167,23 @@
                     jnp.concatenate(sides, axis=1)
                 )
 
+    def windowed(planes, pair, first):
+        left = jnp.concatenate(
+            [
+                plane[:, column * 128 : (column + 1) * 128]
+                for plane in planes
+                for column in (pair, (pair + 1) % 4)
+            ],
+            axis=1,
+        )
+        return jnp.dot(left, taps[first : first + 256 * len(planes)], preferred_element_type=f32)
+
+    for p, own, first in ((0, (0, 2), 256), (1, (1, 3), 256), (2, (0, 2), 0), (3, (1, 3), 0), (4, (2,), 0)):
+        planes = [fields_ref[x] for x in own]
+        for pair in range(4):
+            partial[p * 4 + pair] = windowed(planes, pair, first)
+    prepare()
+
     asked_finish()
     table = asked[...]
 
@@ -192,23 +210,14 @@
 
     conv_bias = jnp.concatenate([conv_bias_ref[...], conv_bias_ref[...]], axis=1)
     arrived = set()
-
-    def plane_pair(x, pair):
-        columns = slice(pair * 128, (pair + 1) * 128)
-        if 0 <= x < 4:
-            return fields_ref[x][:, columns]
-        slot = x + 2 if x < 0 else x - 2
-        if slot not in arrived:
-            arrived.add(slot)
-            halo_copies[slot].wait()
-        return halo[slot][:, columns]
-
-    for p in (2, 0, 1, 3, 4):
+    for p, slots_in, first in ((0, (0,), 0), (2, (2,), 512), (1, (1,), 0), (3, (3,), 512), (4, (2, 4), 256)):
+        for slot in slots_in:
+            if slot not in arrived:
+                arrived.add(slot)
+                halo_copies[slot].wait()
+        planes = [halo[slot] for slot in slots_in]
         for pair in range(4):
-            left = jnp.concatenate(
-                [plane_pair(p + 2 * dx, (pair + k) % 4) for dx in (-1, 0, 1) for k in (0, 1)], axis=1
-            )
-            mixed = jnp.dot(left, taps[...], preferred_element_type=f32)
+            mixed = partial[p * 4 + pair] + windowed(planes, pair, first)
             v = (
                 mixed[:, 128:256]
                 + pltpu.roll(mixed[:, 0:128], 1, axis=0)
@@ -236,7 +245,7 @@
     act_high, act_low, cot_high, cot_low,
     pair_send, pair_recv, plane_send, plane_recv, zs_send, zs_recv, zg_send, zg_recv,
     pg_send, pg_recv, cg_send, cg_recv,
-    w_mid_buf, w_mid_sem,
+    w_mid_buf, w_mid_sem, mid_high, mid_low, turned_high, turned_low,
     *encode_scratch,
 ):
     n_z, n_tile, query_total = sizes
@@ -267,10 +276,16 @@
     for z_index in depths:
         pl.semaphore_signal(barrier, inc=1, device_id=at_z(z_index), device_id_type=MESH)
     pl.semaphore_wait(barrier, n_tile + n_z - 2)
+    def prepare():
+        w_mid_copy.wait()
+        mid_high[...], mid_low[...] = halves(w_mid_buf[...])
+        turned_high[...], turned_low[...] = halves(jnp.transpose(w_mid_buf[...]))
+
     latent_rows, position = encode_part(
         (z, tile, n_tile),
         (fields_ref, weight_ref, conv_bias_ref, owner_ref, cell_ref, frac_ref),
         encode_scratch,
+        prepare,
     )
 
     w_pos = w_pos_ref[...]
@@ -293,8 +308,7 @@
     for d in range(3):
         keep(act_high, act_low, 1 + d, slope_one * w_pos[d : d + 1])
     keep(act_high, act_low, 4, curve_one * pos_square)
-    w_mid_copy.wait()
-    w_mid = halves(w_mid_buf[...])
+    w_mid = (mid_high[...], mid_low[...])
 
     def mixed(k):
         rows = slice(k * 128, (k + 1) * 128)
@@ -393,6 +407,45 @@
     keep(cot_high, cot_low, 0, d_sum_two)
     grad_bias_two = jnp.sum(d_sum_two, axis=0, keepdims=True)
 
+    def back(k):
+        rows = slice(k * 128, (k + 1) * 128)
+        return product((cot_high[rows], cot_low[rows]), (turned_high[...], turned_low[...]), NN)
+
+    d_act_one = back(0)
+    d_slope_one = jnp.zeros_like(slope_one)
+    second_back = back(4)
+    second_sum = 2.0 * jnp.sum(second_back * curve_one, axis=0, keepdims=True)
+    grad_pos = []
+    for d in range(3):
+        tangent_back = back(1 + d)
+        d_slope_one = d_slope_one + tangent_back * w_pos[d : d + 1]
+        grad_pos.append(
+            jnp.sum(tangent_back * slope_one, axis=0, keepdims=True)
+            + w_pos[d : d + 1] * second_sum
+        )
+    d_curve_one = second_back * pos_square
+    d_slope_one = d_slope_one - 2.0 * act_one * d_curve_one
+    d_sum_one = slope_one * (
+        d_act_one - 2.0 * slope_one * d_curve_one - 2.0 * act_one * d_slope_one
+    )
+    for d in range(3):
+        grad_pos[d] = grad_pos[d] + jnp.sum(
+            d_sum_one * position[d], axis=0, keepdims=True
+        )
+    grad_bias_one = jnp.sum(d_sum_one, axis=0, keepdims=True)
+    sum_high, sum_low = halves(d_sum_one)
+    grad_latent = lax.dot_general(
+        latent_rows, sum_high, (TN, ((), ())), preferred_element_type=f32
+    ) + lax.dot_general(latent_rows, sum_low, (TN, ((), ())), preferred_element_type=f32)
+    small = jnp.concatenate(
+        grad_pos + [grad_bias_one, grad_bias_two, jnp.zeros((3, 512), f32), grad_out, jnp.zeros((3, 512), f32)],
+        axis=0,
+    )
+    grads[9] = jnp.zeros((256, 128), f32)
+    for j in range(4):
+        grads[8, j * 64 : (j + 1) * 64] = grad_latent[:, j * 128 : (j + 1) * 128]
+        grads[9, j * 64 : j * 64 + 16] = small[:, j * 128 : (j + 1) * 128]
+    grads[9, 16:24] = jnp.concatenate([d_value, loss_row, jnp.zeros((2, 128), f32)], axis=0)
     def pair_copy(first, count, slot):
         rows = pl.ds(pl.multiple_of(other * 128, 128), 128)
         return pltpu.make_async_remote_copy(
@@ -404,101 +457,50 @@
             device_id_type=MESH,
         )
 
-    pair_copies = []
-    for p in range(8):
-        r, c = (p // 4) * 256, (p % 4) * 128
-        grads[p] = product(
-            (act_high[:, r : r + 256], act_low[:, r : r + 256]),
-            (cot_high[:, c : c + 128], cot_low[:, c : c + 128]),
-            TN,
-        )
-        copy = pair_copy(p, 1, p)
-        copy.start()
-        pair_copies.append(copy)
+    pair_copies = [pair_copy(8, 2, 2), pair_copy(0, 4, 0), pair_copy(4, 4, 1)]
+    pair_copies[0].start()
+
+    for half in range(2):
+        r = half * 256
+        block = product(
+            (act_high[:, r : r + 256], act_low[:, r : r + 256]), (cot_high[...], cot_low[...]), TN
+        )
+        for k in range(4):
+            grads[half * 4 + k] = block[:, k * 128 : (k + 1) * 128]
+        pair_copies[1 + half].start()
 
     mine = pl.ds(pl.multiple_of(core * 128, 128), 128)
 
-    def plane_copies(first, count, group):
-        copies = []
-        for chip_index in chips:
-            rows = pl.ds(pl.multiple_of(core * 128 + chip_index * rows_xy, 8), rows_xy)
-            copies.append(
-                pltpu.make_async_remote_copy(
-                    src_ref=grads.at[pl.ds(first, count), rows],
-                    dst_ref=plane_buf.at[chip, pl.ds(first, count)],
-                    send_sem=plane_send.at[group],
-                    recv_sem=plane_recv.at[group],
-                    device_id=at_tile(chip_index, core),
-                    device_id_type=MESH,
-                )
-            )
-        return copies
-
-    for p in range(8):
-        pair_copies[p].wait()
-        grads[p, mine] = grads[p, mine] + pair_buf[p]
-    first_group = plane_copies(0, 8, 0)
-    for copy in first_group:
-        copy.start()
-
-    def back(k):
-        rows = slice(k * 128, (k + 1) * 128)
-        return product((cot_high[rows], cot_low[rows]), w_mid, NT)
-
-    d_act_one = back(0)
-    d_slope_one = jnp.zeros_like(slope_one)
-    second_back = back(4)
-    second_sum = 2.0 * jnp.sum(second_back * curve_one, axis=0, keepdims=True)
-    grad_pos = []
-    for d in range(3):
-        tangent_back = back(1 + d)
-        d_slope_one = d_slope_one + tangent_back * w_pos[d : d + 1]
-        grad_pos.append(
-            jnp.sum(tangent_back * slope_one, axis=0, keepdims=True)
-            + w_pos[d : d + 1] * second_sum
-        )
-    d_curve_one = second_back * pos_square
-    d_slope_one = d_slope_one - 2.0 * act_one * d_curve_one
-    d_sum_one = slope_one * (
-        d_act_one - 2.0 * slope_one * d_curve_one - 2.0 * act_one * d_slope_one
-    )
-    for d in range(3):
-        grad_pos[d] = grad_pos[d] + jnp.sum(
-            d_sum_one * position[d], axis=0, keepdims=True
-        )
-    grad_bias_one = jnp.sum(d_sum_one, axis=0, keepdims=True)
-    sum_high, sum_low = halves(d_sum_one)
-    grad_latent = lax.dot_general(
-        latent_rows, sum_high, (TN, ((), ())), preferred_element_type=f32
-    ) + lax.dot_general(latent_rows, sum_low, (TN, ((), ())), preferred_element_type=f32)
-    small = jnp.concatenate(
-        grad_pos + [grad_bias_one, grad_bias_two, jnp.zeros((3, 512), f32), grad_out, jnp.zeros((3, 512), f32)],
-        axis=0,
-    )
-    grads[9] = jnp.zeros((256, 128), f32)
-    for j in range(4):
-        grads[8, j * 64 : (j + 1) * 64] = grad_latent[:, j * 128 : (j + 1) * 128]
-        grads[9, j * 64 : j * 64 + 16] = small[:, j * 128 : (j + 1) * 128]
-    grads[9, 16:24] = jnp.concatenate([d_value, loss_row, jnp.zeros((2, 128), f32)], axis=0)
-    last_pair = pair_copy(8, 2, 8)
-    last_pair.start()
-    last_pair.wait()
-    for p in (8, 9):
-        grads[p, mine] = grads[p, mine] + pair_buf[p]
-    second_group = plane_copies(8, 2, 1)
-    for copy in second_group:
-        copy.start()
-
-    for group, first, count in ((0, 0, 8), (1, 8, 2)):
-        block = plane_buf.at[pl.ds(0, n_xy - 1), pl.ds(first, count)]
+    def pair_sum(planes):
+        for p in planes:
+            grads[p, mine] = grads[p, mine] + pair_buf[p]
+
+    pair_copies[0].wait()
+    pair_sum((8, 9))
+    pair_copies[1].wait()
+    pair_sum((0, 1, 2, 3))
+    pair_copies[2].wait()
+    pair_sum((4, 5, 6, 7))
+    for chip_index in chips:
+        rows = pl.ds(pl.multiple_of(core * 128 + chip_index * rows_xy, 8), rows_xy)
         pltpu.make_async_remote_copy(
-            src_ref=block,
-            dst_ref=block,
-            send_sem=plane_send.at[group],
-            recv_sem=plane_recv.at[group],
-            device_id=at_tile(chip, other),
+            src_ref=grads.at[:, rows],
+            dst_ref=plane_buf.at[chip],
+            send_sem=plane_send,
+            recv_sem=plane_recv,
+            device_id=at_tile(chip_index, core),
             device_id_type=MESH,
-        ).wait()
+        ).start()
+
+    block = plane_buf.at[pl.ds(0, n_xy - 1)]
+    pltpu.make_async_remote_copy(
+        src_ref=block,
+        dst_ref=block,
+        send_sem=plane_send,
+        recv_sem=plane_recv,
+        device_id=at_tile(chip, other),
+        device_id_type=MESH,
+    ).wait()
     own = pl.ds(pl.multiple_of(core * 128 + chip * rows_xy, 8), rows_xy)
     total = grads[:, own]
     for chip_index in chips:
@@ -624,16 +626,21 @@
             pltpu.VMEM((640, hidden), bf16),
             pltpu.VMEM((640, hidden), bf16),
             pltpu.VMEM((640, hidden), bf16),
-            DMA((9,)), DMA((9,)),
-            DMA((2,)), DMA((2,)),
+            DMA((3,)), DMA((3,)),
+            DMA(()), DMA(()),
             DMA(()), DMA(()),
             DMA(()), DMA(()),
             DMA(()), DMA((n_xy,)),
             DMA(()), DMA(()),
             pltpu.VMEM((hidden, hidden), f32),
             DMA(()),
+            pltpu.VMEM((hidden, hidden), bf16),
+            pltpu.VMEM((hidden, hidden), bf16),
+            pltpu.VMEM((hidden, hidden), bf16),
+            pltpu.VMEM((hidden, hidden), bf16),
             pltpu.VMEM((5, 128, 512), bf16),
             pltpu.VMEM((768, 384), bf16),
+            pltpu.VMEM((20, 128, 384), f32),
             pltpu.VMEM((2560, 128), bf16),
             pltpu.VMEM((2, 256, 2560), bf16),
             pltpu.VMEM((256, 128), f32),

time: 73.5 us -> 67.9 us (0.924)
  Pallas kernels: 70.1 us -> 64.4 us
    pallas_call x1, Pallas kernels: 68.4 us -> 62.7 us  [whole_step(): pl.pallas_call(functools.partial(step_kernel, sizes), out_shape=(jax.Shap...]
where the time goes in v2:
time: 67.9 us; the launch traced here: 67.7 us
  Pallas kernels  64.4 us (95%)
  local copies, waits for them, and re-layouts  2.39 us (4%)
  between operations  0.84 us (1%)
    pallas_call x1, Pallas kernels, whole_step(): pl.pallas_call(functools.partial(step_kernel, sizes), out_shape=(jax.Shap...  62.7 us
    unnamed x27, local copies, waits for them, and re-layouts  2.13 us
    pallas_call x1, Pallas kernels, unpacked(): pl.pallas_call(unpack_kernel, out_shape=tuple((jax.ShapeDtypeStruct(shape...  1.7 us

profile of v2, /device:TPU:1, one launch (start us, length us, event | category | flops | bytes accessed | tf_op | source)
XLA Modules:
  0.0 67.7 jit_solution(8634013595001131607)
XLA Ops:
  0.6 1.2 %copy.27 = bf16[1,64,4,8,128]{4,1,3,2,0:T(8,128)(2,1)S(1)} copy(bf16[1,64,4,8,128]{4,3,2,1,0:T(8,128)(2,1)} %param.14) | data formatting | bytes 1048576 | tf_op args[0]
  1.9 0.0 copy-start
  1.9 0.0 copy-start.1
  1.9 0.0 copy-start.2
  1.9 0.0 copy-start.3
  2.0 0.0 copy-start.4
  2.0 0.0 copy-start.5
  2.0 0.0 copy-start.6
  2.0 0.0 copy-start.7
  2.0 0.0 copy-start.8
  2.0 0.0 copy-start.9
  2.0 0.0 copy-start.10
  2.0 0.0 copy-start.11
  2.0 0.0 copy-start.12
  2.2 0.2 copy.25.fields_ref
  2.4 0.7 %copy-done = f32[512,512]{1,0:T(8,128)S(1)} copy-done((f32[512,512]{1,0:T(8,128)S(1)}, f32[512,512]{1,0:T(8,128)}, u32[]{:S(2)}) %copy-start) | copy-done | bytes 1048600
  3.1 0.0 copy-done.1
  3.2 0.0 copy-done.2
  3.2 0.0 copy-done.3
  3.2 0.0 copy-done.4
  3.2 0.0 copy-done.5
  3.2 0.0 copy-done.6
  3.2 0.0 copy-done.7
  3.2 0.0 copy-done.8
  3.2 0.0 copy-done.9
  3.2 0.0 copy-done.10
  3.2 0.0 copy-done.11
  3.3 0.0 copy-done.12
  3.3 62.7 %step.1 = (f32[5,1,128]{2,1,0:T(1,128)S(1)}, f32[10,256,128]{2,1,0:T(8,128)S(1)}) custom-call(bf16[4,128,512]{2,1,0:T(8,128)(2,1)S(1)} %copy.25.fields_ref, bf16[64,1728]{1,0:T(8,128)(2,1)S(1)} %copy-done.1, f32[1,64]{1,0:T(1,128)S(1)} %bitcast.22, s32[1,128]{1,0:T(1,128)S(1)} %bitcast.23, s32[1,128]{1,0:T(1,128)S(1)} %copy-done.11, ...), custom_call_target="tpu_custom_call" | custom-call | tf_op jit(solution)/shard_map/step/pallas_call | solution.py:607
  66.0 1.7 %unpack.1 = (f32[5,1,128]{2,1,0:T(1,128)}, f32[64,512]{1,0:T(8,128)}, f32[3,512]{1,0:T(4,128)}, f32[1,512]{1,0:T(1,128)}, f32[512,512]{1,0:T(8,128)}, /*index=5*...) custom-call(f32[5,1,128]{2,1,0:T(1,128)S(1)} %get-tuple-element.20.prediction_ref, ...), custom_call_target="tpu_custom_call" | custom-call | tf_op jit(solution)/shard_map/unpack/pallas_call | solution.py:696
  (3 shorter events, 0.1 us)
Async XLA Ops:
  1.9 1.2 %copy-start = (f32[512,512]{1,0:T(8,128)S(1)}, f32[512,512]{1,0:T(8,128)}, u32[]{:S(2)}) copy-start(f32[512,512]{1,0:T(8,128)} %w_mid_ref.1) | copy-start | bytes 3145732
  1.9 1.2 %copy-start.1 = (bf16[64,1728]{1,0:T(8,128)(2,1)S(1)}, bf16[64,1728]{1,0:T(8,128)(2,1)}, u32[]{:S(2)}) copy-start(bf16[64,1728]{1,0:T(8,128)(2,1)} %weight_ref.1) | copy-start | bytes 663556
  1.9 1.3 %copy-start.2 = (f32[64,512]{1,0:T(8,128)S(1)}, f32[64,512]{1,0:T(8,128)}, u32[]{:S(2)}) copy-start(f32[64,512]{1,0:T(8,128)} %w_latent_ref.1) | copy-start | bytes 393220
  1.9 1.3 %copy-start.3 = (f32[5,512]{1,0:T(8,128)S(1)}, f32[5,512]{1,0:T(8,128)}, u32[]{:S(2)}) copy-start(f32[5,512]{1,0:T(8,128)} %w_out_ref.1) | copy-start | bytes 30724
  2.0 1.2 %copy-start.4 = (f32[3,512]{1,0:T(4,128)S(1)}, f32[3,512]{1,0:T(4,128)}, u32[]{:S(2)}) copy-start(f32[3,512]{1,0:T(4,128)} %w_pos_ref.1) | copy-start | bytes 18436
  2.0 1.2 %copy-start.5 = (f32[1,5,128]{2,0,1:T(1,128)S(1)}, f32[1,5,128]{2,0,1:T(1,128)}, u32[]{:S(2)}) copy-start(f32[1,5,128]{2,0,1:T(1,128)} %param.20) | copy-start | bytes 7684
  2.0 1.2 %copy-start.6 = (f32[512]{0:T(512)S(1)}, f32[512]{0:T(512)}, u32[]{:S(2)}) copy-start(f32[512]{0:T(512)} %param.23) | copy-start | bytes 6148
  2.0 1.2 %copy-start.7 = (f32[512]{0:T(512)S(1)}, f32[512]{0:T(512)}, u32[]{:S(2)}) copy-start(f32[512]{0:T(512)} %param.25) | copy-start | bytes 6148
  2.0 1.2 %copy-start.8 = (f32[1,3,128]{2,0,1:T(1,128)S(1)}, f32[1,3,128]{2,0,1:T(1,128)}, u32[]{:S(2)}) copy-start(f32[1,3,128]{2,0,1:T(1,128)} %param.19) | copy-start | bytes 4612
  2.0 1.2 %copy-start.9 = (f32[64]{0:T(128)S(1)}, f32[64]{0:T(128)}, u32[]{:S(2)}) copy-start(f32[64]{0:T(128)} %param.16) | copy-start | bytes 772
  2.0 1.2 %copy-start.10 = (s32[1,128,1]{1,2,0:T(1,128)S(1)}, s32[1,128,1]{1,2,0:T(1,128)}, u32[]{:S(2)}) copy-start(s32[1,128,1]{1,2,0:T(1,128)} %param.17) | copy-start | bytes 1540
  2.0 1.2 %copy-start.11 = (s32[1,128]{1,0:T(1,128)S(1)}, s32[1,128]{1,0:T(1,128)}, u32[]{:S(2)}) copy-start(s32[1,128]{1,0:T(1,128)} %cell_ref.1) | copy-start | bytes 1540
  2.0 1.2 %copy-start.12 = (f32[5]{0:T(128)S(1)}, f32[5]{0:T(128)}, u32[]{:S(2)}) copy-start(f32[5]{0:T(128)} %param.27) | copy-start | bytes 64

commit v3 on v2

--- a/solution.py
+++ b/solution.py
@@ -15,6 +15,7 @@
 
 MESH = pl.DeviceIdType.MESH
 PLANES = 10
+GROUPS = ((0, 6), (6, 4))
 f32 = jnp.float32
 bf16 = jnp.bfloat16
 
@@ -38,12 +39,32 @@
 
 
 NN = ((1,), (0,))
+
+
+def hops(step, length):
+    return min(step, length - step)
+
+
+def others_along(index, length):
+    steps = sorted(range(1, length), key=lambda step: -hops(step, length))
+    return [lax.rem(index + step, length) for step in steps]
+
+
+def other_chips(chip, count):
+    columns = 4 if count % 4 == 0 else count
+    rows = count // columns
+    x, y = lax.rem(chip, columns), chip // columns
+    steps = [(i, j) for i in range(rows) for j in range(columns) if i or j]
+    steps.sort(key=lambda step: -hops(step[0], rows) - hops(step[1], columns))
+    return [lax.rem(y + i, rows) * columns + lax.rem(x + j, columns) for i, j in steps]
+
+
 NT = ((1,), (1,))
 TN = ((0,), (0,))
 
 
 def encode_part(place, refs, scratch, prepare):
-    z, tile, n_tile = place
+    z, tile, n_tile, others = place
     fields_ref, weight_ref, conv_bias_ref, owner_ref, cell_ref, frac_ref = refs
     (
         halo, taps, partial, latent, corner, asked, wanted, answer, answered,
@@ -51,7 +72,6 @@
     ) = scratch
     slots = 256 // n_tile
     above, below = lax.rem(tile + 1, n_tile), lax.rem(tile + n_tile - 1, n_tile)
-    others = [lax.rem(tile + step, n_tile) for step in range(1, n_tile)]
 
     def at_tile(index):
         return {"replica": z, "tile": index}
@@ -241,13 +261,14 @@
     target_ref, w_latent_ref, w_pos_ref, bias_one_ref, w_mid_ref,
     bias_two_ref, w_out_ref, bias_out_ref,
     prediction_ref, packed_ref,
-    grads, pair_buf, plane_buf, z_send, z_buf, z_all, piece,
+    grads, pair_buf, plane_buf, z_send_0, z_send_1, z_buf_0, z_buf_1, z_all_0, z_all_1, piece,
     act_high, act_low, cot_high, cot_low,
     pair_send, pair_recv, plane_send, plane_recv, zs_send, zs_recv, zg_send, zg_recv,
     pg_send, pg_recv, cg_send, cg_recv,
     w_mid_buf, w_mid_sem, mid_high, mid_low, turned_high, turned_low,
     *encode_scratch,
 ):
+    z_send, z_buf, z_all = (z_send_0, z_send_1), (z_buf_0, z_buf_1), (z_all_0, z_all_1)
     n_z, n_tile, query_total = sizes
     n_xy = n_tile // 2
     rows_xy = 128 // n_xy
@@ -264,15 +285,14 @@
     def at_z(z_index):
         return {"replica": z_index, "tile": tile}
 
-    chips = [lax.rem(chip + step, n_xy) for step in range(1, n_xy)]
-    depths = [lax.rem(z + step, n_z) for step in range(1, n_z)]
+    chips = other_chips(chip, n_xy)
+    depths = others_along(z, n_z)
+    tiles = [chip_index * 2 + side for chip_index in chips for side in (core, other)] + [chip * 2 + other]
     w_mid_copy = pltpu.make_async_copy(w_mid_ref, w_mid_buf, w_mid_sem)
     w_mid_copy.start()
     barrier = pltpu.get_barrier_semaphore()
-    for step in range(1, n_tile):
-        pl.semaphore_signal(
-            barrier, inc=1, device_id={"replica": z, "tile": lax.rem(tile + step, n_tile)}, device_id_type=MESH
-        )
+    for index in tiles:
+        pl.semaphore_signal(barrier, inc=1, device_id={"replica": z, "tile": index}, device_id_type=MESH)
     for z_index in depths:
         pl.semaphore_signal(barrier, inc=1, device_id=at_z(z_index), device_id_type=MESH)
     pl.semaphore_wait(barrier, n_tile + n_z - 2)
@@ -282,7 +302,7 @@
         turned_high[...], turned_low[...] = halves(jnp.transpose(w_mid_buf[...]))
 
     latent_rows, position = encode_part(
-        (z, tile, n_tile),
+        (z, tile, n_tile, tiles),
         (fields_ref, weight_ref, conv_bias_ref, owner_ref, cell_ref, frac_ref),
         encode_scratch,
         prepare,
@@ -441,11 +461,11 @@
         grad_pos + [grad_bias_one, grad_bias_two, jnp.zeros((3, 512), f32), grad_out, jnp.zeros((3, 512), f32)],
         axis=0,
     )
-    grads[9] = jnp.zeros((256, 128), f32)
+    grads[1] = jnp.zeros((256, 128), f32)
     for j in range(4):
-        grads[8, j * 64 : (j + 1) * 64] = grad_latent[:, j * 128 : (j + 1) * 128]
-        grads[9, j * 64 : j * 64 + 16] = small[:, j * 128 : (j + 1) * 128]
-    grads[9, 16:24] = jnp.concatenate([d_value, loss_row, jnp.zeros((2, 128), f32)], axis=0)
+        grads[0, j * 64 : (j + 1) * 64] = grad_latent[:, j * 128 : (j + 1) * 128]
+        grads[1, j * 64 : j * 64 + 16] = small[:, j * 128 : (j + 1) * 128]
+    grads[1, 16:24] = jnp.concatenate([d_value, loss_row, jnp.zeros((2, 128), f32)], axis=0)
     def pair_copy(first, count, slot):
         rows = pl.ds(pl.multiple_of(other * 128, 128), 128)
         return pltpu.make_async_remote_copy(
@@ -457,7 +477,7 @@
             device_id_type=MESH,
         )
 
-    pair_copies = [pair_copy(8, 2, 2), pair_copy(0, 4, 0), pair_copy(4, 4, 1)]
+    pair_copies = [pair_copy(0, 2, 2), pair_copy(2, 4, 0), pair_copy(6, 4, 1)]
     pair_copies[0].start()
 
     for half in range(2):
@@ -466,7 +486,7 @@
             (act_high[:, r : r + 256], act_low[:, r : r + 256]), (cot_high[...], cot_low[...]), TN
         )
         for k in range(4):
-            grads[half * 4 + k] = block[:, k * 128 : (k + 1) * 128]
+            grads[2 + half * 4 + k] = block[:, k * 128 : (k + 1) * 128]
         pair_copies[1 + half].start()
 
     mine = pl.ds(pl.multiple_of(core * 128, 128), 128)
@@ -475,42 +495,43 @@
         for p in planes:
             grads[p, mine] = grads[p, mine] + pair_buf[p]
 
-    pair_copies[0].wait()
-    pair_sum((8, 9))
-    pair_copies[1].wait()
-    pair_sum((0, 1, 2, 3))
-    pair_copies[2].wait()
-    pair_sum((4, 5, 6, 7))
-    for chip_index in chips:
-        rows = pl.ds(pl.multiple_of(core * 128 + chip_index * rows_xy, 8), rows_xy)
-        pltpu.make_async_remote_copy(
-            src_ref=grads.at[:, rows],
-            dst_ref=plane_buf.at[chip],
-            send_sem=plane_send,
-            recv_sem=plane_recv,
-            device_id=at_tile(chip_index, core),
+    def plane_rows(chip_index):
+        return pl.ds(pl.multiple_of(core * 128 + chip_index * rows_xy, 8), rows_xy)
+
+    def finish(block, send_sem, recv_sem):
+        return pltpu.make_async_remote_copy(
+            src_ref=block,
+            dst_ref=block,
+            send_sem=send_sem,
+            recv_sem=recv_sem,
+            device_id=at_tile(chip, other),
             device_id_type=MESH,
-        ).start()
-
-    block = plane_buf.at[pl.ds(0, n_xy - 1)]
-    pltpu.make_async_remote_copy(
-        src_ref=block,
-        dst_ref=block,
-        send_sem=plane_send,
-        recv_sem=plane_recv,
-        device_id=at_tile(chip, other),
-        device_id_type=MESH,
-    ).wait()
-    own = pl.ds(pl.multiple_of(core * 128 + chip * rows_xy, 8), rows_xy)
-    total = grads[:, own]
-    for chip_index in chips:
-        total = total + plane_buf[chip_index]
-
-    for k in range(n_z):
-        for p in range(PLANES):
-            z_send[k, p * rows_z : (p + 1) * rows_z] = total[p, k * rows_z : (k + 1) * rows_z]
-
-    def exchange(source, target, send_sem, recv_sem):
+        )
+
+    def start_plane_sum(group):
+        for chip_index in chips:
+            pltpu.make_async_remote_copy(
+                src_ref=grads.at[pl.ds(*GROUPS[group]), plane_rows(chip_index)],
+                dst_ref=plane_buf.at[chip, pl.ds(*GROUPS[group])],
+                send_sem=plane_send.at[group],
+                recv_sem=plane_recv.at[group],
+                device_id=at_tile(chip_index, core),
+                device_id_type=MESH,
+            ).start()
+
+    def plane_sum(group):
+        first, count = GROUPS[group]
+        finish(
+            plane_buf.at[pl.ds(0, n_xy - 1), pl.ds(first, count)], plane_send.at[group], plane_recv.at[group]
+        ).wait()
+        total = grads[first : first + count, plane_rows(chip)]
+        for chip_index in chips:
+            total = total + plane_buf[chip_index, first : first + count]
+        for k in range(n_z):
+            for p in range(count):
+                z_send[group][k, p * rows_z : (p + 1) * rows_z] = total[p, k * rows_z : (k + 1) * rows_z]
+
+    def start_exchange(source, target, send_sem, recv_sem):
         for z_index in depths:
             pltpu.make_async_remote_copy(
                 src_ref=source(z_index),
@@ -520,79 +541,66 @@
                 device_id=at_z(z_index),
                 device_id_type=MESH,
             ).start()
-        block = target.at[pl.ds(0, n_z - 1)]
-        pltpu.make_async_remote_copy(
-            src_ref=block,
-            dst_ref=block,
-            send_sem=send_sem,
-            recv_sem=recv_sem,
-            device_id=at_tile(chip, other),
-            device_id_type=MESH,
+
+    def start_z_sum(group):
+        start_exchange(
+            lambda z_index: z_send[group].at[z_index], z_buf[group], zs_send.at[group], zs_recv.at[group]
+        )
+
+    def z_sum(group):
+        finish(z_buf[group].at[pl.ds(0, n_z - 1)], zs_send.at[group], zs_recv.at[group]).wait()
+        reduced = z_send[group][z]
+        for z_index in depths:
+            reduced = reduced + z_buf[group][z_index]
+        z_all[group][z] = reduced
+        start_exchange(lambda z_index: z_all[group].at[z], z_all[group], zg_send.at[group], zg_recv.at[group])
+
+    def start_gather(group):
+        first, count = GROUPS[group]
+        finish(z_all[group].at[pl.ds(0, n_z - 1)], zg_send.at[group], zg_recv.at[group]).wait()
+        for k in range(n_z):
+            for p in range(count):
+                piece[first + p, k * rows_z : (k + 1) * rows_z] = z_all[group][k, p * rows_z : (p + 1) * rows_z]
+        for chip_index in chips:
+            pltpu.make_async_remote_copy(
+                src_ref=piece.at[pl.ds(first, count)],
+                dst_ref=packed_ref.at[pl.ds(first, count), plane_rows(chip)],
+                send_sem=pg_send.at[group],
+                recv_sem=pg_recv.at[group],
+                device_id=at_tile(chip_index, core),
+                device_id_type=MESH,
+            ).start()
+        packed_ref[first : first + count, plane_rows(chip)] = piece[first : first + count]
+
+    def cross(group):
+        first, count = GROUPS[group]
+        finish(
+            packed_ref.at[pl.ds(first, count), pl.ds(0, (n_xy - 1) * rows_xy)], pg_send.at[group], pg_recv.at[group]
         ).wait()
-
-    exchange(lambda z_index: z_send.at[z_index], z_buf, zs_send, zs_recv)
-    reduced = z_send[z]
-    for z_index in depths:
-        reduced = reduced + z_buf[z_index]
-    z_all[z] = reduced
-    exchange(lambda z_index: z_all.at[z], z_all, zg_send, zg_recv)
-
-    for k in range(n_z):
-        for p in range(PLANES):
-            piece[p, k * rows_z : (k + 1) * rows_z] = z_all[k, p * rows_z : (p + 1) * rows_z]
-    packed_ref[:, own] = piece[...]
-    for chip_index in chips:
-        copy = pltpu.make_async_remote_copy(
-            src_ref=piece,
-            dst_ref=packed_ref.at[:, own],
-            send_sem=pg_send,
-            recv_sem=pg_recv.at[chip],
-            device_id=at_tile(chip_index, core),
-            device_id_type=MESH,
-        )
+        half = packed_ref.at[pl.ds(first, count), mine]
+        copy = finish(half, cg_send.at[group], cg_recv.at[group])
         copy.start()
-
-    def cross(chip_index):
-        rows = pl.ds(pl.multiple_of(core * 128 + chip_index * rows_xy, 8), rows_xy)
-        return pltpu.make_async_remote_copy(
-            src_ref=packed_ref.at[:, rows],
-            dst_ref=packed_ref.at[:, rows],
-            send_sem=cg_send,
-            recv_sem=cg_recv,
-            device_id=at_tile(chip, other),
-            device_id_type=MESH,
-        )
-
-    cross(chip).start()
-    for chip_index in chips:
-        rows = pl.ds(pl.multiple_of(core * 128 + chip_index * rows_xy, 8), rows_xy)
-        pltpu.make_async_remote_copy(
-            src_ref=piece,
-            dst_ref=packed_ref.at[:, rows],
-            send_sem=pg_send,
-            recv_sem=pg_recv.at[chip_index],
-            device_id=at_tile(chip_index, core),
-            device_id_type=MESH,
-        ).wait_recv()
-        cross(chip_index).start()
-    half = packed_ref.at[:, pl.ds(0, (n_xy - 1) * rows_xy)]
-    pltpu.make_async_remote_copy(
-        src_ref=half,
-        dst_ref=half,
-        send_sem=pg_send,
-        recv_sem=pg_recv.at[chip],
-        device_id=at_tile(chip, other),
-        device_id_type=MESH,
-    ).wait_send()
-    half = packed_ref.at[:, pl.ds(0, 128)]
-    pltpu.make_async_remote_copy(
-        src_ref=half,
-        dst_ref=half,
-        send_sem=cg_send,
-        recv_sem=cg_recv,
-        device_id=at_tile(chip, other),
-        device_id_type=MESH,
-    ).wait()
+        return copy
+
+    pair_copies[0].wait()
+    pair_sum((0, 1))
+    pair_copies[1].wait()
+    pair_sum((2, 3, 4, 5))
+    start_plane_sum(0)
+    pair_copies[2].wait()
+    pair_sum((6, 7, 8, 9))
+    start_plane_sum(1)
+    plane_sum(0)
+    start_z_sum(0)
+    plane_sum(1)
+    start_z_sum(1)
+    z_sum(0)
+    z_sum(1)
+    start_gather(0)
+    start_gather(1)
+    crossed = [cross(0), cross(1)]
+    for copy in crossed:
+        copy.wait()
 
 
 def whole_step(
@@ -618,20 +626,23 @@
             pltpu.VMEM((PLANES, 256, 128), f32),
             pltpu.VMEM((PLANES, 128, 128), f32),
             pltpu.VMEM((n_xy, PLANES, rows_xy, 128), f32),
-            pltpu.VMEM((n_z, PLANES * rows_z, 128), f32),
-            pltpu.VMEM((n_z, PLANES * rows_z, 128), f32),
-            pltpu.VMEM((n_z, PLANES * rows_z, 128), f32),
+            pltpu.VMEM((n_z, 6 * rows_z, 128), f32),
+            pltpu.VMEM((n_z, 4 * rows_z, 128), f32),
+            pltpu.VMEM((n_z, 6 * rows_z, 128), f32),
+            pltpu.VMEM((n_z, 4 * rows_z, 128), f32),
+            pltpu.VMEM((n_z, 6 * rows_z, 128), f32),
+            pltpu.VMEM((n_z, 4 * rows_z, 128), f32),
             pltpu.VMEM((PLANES, rows_xy, 128), f32),
             pltpu.VMEM((640, hidden), bf16),
             pltpu.VMEM((640, hidden), bf16),
             pltpu.VMEM((640, hidden), bf16),
             pltpu.VMEM((640, hidden), bf16),
             DMA((3,)), DMA((3,)),
-            DMA(()), DMA(()),
-            DMA(()), DMA(()),
-            DMA(()), DMA(()),
-            DMA(()), DMA((n_xy,)),
-            DMA(()), DMA(()),
+            DMA((2,)), DMA((2,)),
+            DMA((2,)), DMA((2,)),
+            DMA((2,)), DMA((2,)),
+            DMA((2,)), DMA((2,)),
+            DMA((2,)), DMA((2,)),
             pltpu.VMEM((hidden, hidden), f32),
             DMA(()),
             pltpu.VMEM((hidden, hidden), bf16),
@@ -656,7 +667,8 @@
         ),
         name="step",
     )(
-        fields, weight, conv_bias.reshape(1, -1), owner, cell, frac, target, w_latent, w_pos, bias_one.reshape(1, -1), w_mid,
+        fields, weight, conv_bias.reshape(1, -1), owner, cell, frac, target, w_latent, w_pos, bias_one.reshape(1, -1),
+        pltpu.with_memory_space_constraint(w_mid, pltpu.HBM),
         bias_two.reshape(1, -1), w_out, bias_out.reshape(1, -1),
     )
 
@@ -668,20 +680,20 @@
     for p in range(8):
         r, c = (p // 4) * 256, (p % 4) * 128
         copies.append(
-            pltpu.make_async_copy(packed_ref.at[p], mid_ref.at[pl.ds(r, 256), pl.ds(c, 128)], sem.at[p])
+            pltpu.make_async_copy(packed_ref.at[2 + p], mid_ref.at[pl.ds(r, 256), pl.ds(c, 128)], sem.at[p])
         )
     for copy in copies:
         copy.start()
     value_ref[...] = prediction_ref[...]
     for j in range(4):
         columns = slice(j * 128, (j + 1) * 128)
-        latent_ref[:, columns] = packed_ref[8, j * 64 : (j + 1) * 64]
-        small = packed_ref[9, j * 64 : j * 64 + 16]
+        latent_ref[:, columns] = packed_ref[0, j * 64 : (j + 1) * 64]
+        small = packed_ref[1, j * 64 : j * 64 + 16]
         pos_ref[:, columns] = small[0:3]
         one_ref[:, columns] = small[3:4]
         two_ref[:, columns] = small[4:5]
         out_ref[:, columns] = small[8:13]
-    sums = jnp.sum(packed_ref[9, 16:24], axis=1, keepdims=True)
+    sums = jnp.sum(packed_ref[1, 16:24], axis=1, keepdims=True)
     loss_ref[...] = sums[5:6]
     diagonal = lax.broadcasted_iota(jnp.int32, (8, 128), 0) == lax.broadcasted_iota(jnp.int32, (8, 128), 1)
     bias_ref[...] = jnp.sum(

time: 67.9 us -> 63.5 us (0.935)
  Pallas kernels: 64.4 us -> 60.4 us
    pallas_call x1, Pallas kernels: 62.7 us -> 58.7 us  [whole_step(): pl.pallas_call(functools.partial(step_kernel, sizes), out_shape=(jax.Shap...]
    unnamed x27 -> x25, local copies, waits for them, and re-layouts: 2.13 us -> 1.87 us
where the time goes in v3:
time: 63.5 us; the launch traced here: 63.4 us
  Pallas kernels  60.4 us (95%)
  local copies, waits for them, and re-layouts  2.13 us (3%)
  between operations  0.83 us (1%)
    pallas_call x1, Pallas kernels, whole_step(): pl.pallas_call(functools.partial(step_kernel, sizes), out_shape=(jax.Shap...  58.7 us
    unnamed x25, local copies, waits for them, and re-layouts  1.87 us
    pallas_call x1, Pallas kernels, unpacked(): pl.pallas_call(unpack_kernel, out_shape=tuple((jax.ShapeDtypeStruct(shape...  1.7 us

profile of v3, /device:TPU:1, one launch (start us, length us, event | category | flops | bytes accessed | tf_op | source)
XLA Modules:
  0.0 63.4 jit_solution(2870381181717418549)
XLA Ops:
  0.6 1.2 %copy.27 = bf16[1,64,4,8,128]{4,1,3,2,0:T(8,128)(2,1)S(1)} copy(bf16[1,64,4,8,128]{4,3,2,1,0:T(8,128)(2,1)} %param.14) | data formatting | bytes 1048576 | tf_op args[0]
  1.9 0.0 copy-start
  1.9 0.0 copy-start.1
  1.9 0.0 copy-start.2
  1.9 0.0 copy-start.3
  2.0 0.0 copy-start.4
  2.0 0.0 copy-start.5
  2.0 0.0 copy-start.6
  2.0 0.0 copy-start.7
  2.0 0.0 copy-start.8
  2.0 0.0 copy-start.9
  2.0 0.0 copy-start.10
  2.0 0.0 copy-start.11
  2.1 0.2 copy.25.fields_ref
  2.4 0.5 copy-done
  2.8 0.1 copy-done.1
  2.9 0.0 copy-done.2
  2.9 0.0 copy-done.3
  2.9 0.0 copy-done.4
  2.9 0.0 copy-done.5
  2.9 0.0 copy-done.6
  3.0 0.0 copy-done.7
  3.0 0.0 copy-done.8
  3.0 0.0 copy-done.9
  3.0 0.0 copy-done.10
  3.0 0.0 copy-done.11
  3.0 58.7 %step.1 = (f32[5,1,128]{2,1,0:T(1,128)S(1)}, f32[10,256,128]{2,1,0:T(8,128)S(1)}) custom-call(bf16[4,128,512]{2,1,0:T(8,128)(2,1)S(1)} %copy.25.fields_ref, bf16[64,1728]{1,0:T(8,128)(2,1)S(1)} %copy-done, f32[1,64]{1,0:T(1,128)S(1)} %bitcast.22, s32[1,128]{1,0:T(1,128)S(1)} %bitcast.23, s32[1,128]{1,0:T(1,128)S(1)} %copy-done.10, ...), custom_call_target="tpu_custom_call" | custom-call | tf_op jit(solution)/shard_map/step/pallas_call | solution.py:615
  61.7 1.7 %unpack.1 = (f32[5,1,128]{2,1,0:T(1,128)}, f32[64,512]{1,0:T(8,128)}, f32[3,512]{1,0:T(4,128)}, f32[1,512]{1,0:T(1,128)}, f32[512,512]{1,0:T(8,128)}, /*index=5*...) custom-call(f32[5,1,128]{2,1,0:T(1,128)S(1)} %get-tuple-element.20.prediction_ref, ...), custom_call_target="tpu_custom_call" | custom-call | tf_op jit(solution)/shard_map/unpack/pallas_call | solution.py:708
  (3 shorter events, 0.1 us)
Async XLA Ops:
  1.9 0.9 %copy-start = (bf16[64,1728]{1,0:T(8,128)(2,1)S(1)}, bf16[64,1728]{1,0:T(8,128)(2,1)}, u32[]{:S(2)}) copy-start(bf16[64,1728]{1,0:T(8,128)(2,1)} %weight_ref.1) | copy-start | bytes 663556
  1.9 1.0 %copy-start.1 = (f32[64,512]{1,0:T(8,128)S(1)}, f32[64,512]{1,0:T(8,128)}, u32[]{:S(2)}) copy-start(f32[64,512]{1,0:T(8,128)} %w_latent_ref.1) | copy-start | bytes 393220
  1.9 1.0 %copy-start.2 = (f32[5,512]{1,0:T(8,128)S(1)}, f32[5,512]{1,0:T(8,128)}, u32[]{:S(2)}) copy-start(f32[5,512]{1,0:T(8,128)} %w_out_ref.1) | copy-start | bytes 30724
  1.9 1.0 %copy-start.3 = (f32[3,512]{1,0:T(4,128)S(1)}, f32[3,512]{1,0:T(4,128)}, u32[]{:S(2)}) copy-start(f32[3,512]{1,0:T(4,128)} %w_pos_ref.1) | copy-start | bytes 18436
  2.0 1.0 %copy-start.4 = (f32[1,5,128]{2,0,1:T(1,128)S(1)}, f32[1,5,128]{2,0,1:T(1,128)}, u32[]{:S(2)}) copy-start(f32[1,5,128]{2,0,1:T(1,128)} %param.20) | copy-start | bytes 7684
  2.0 1.0 %copy-start.5 = (f32[512]{0:T(512)S(1)}, f32[512]{0:T(512)}, u32[]{:S(2)}) copy-start(f32[512]{0:T(512)} %param.23) | copy-start | bytes 6148
  2.0 1.0 %copy-start.6 = (f32[512]{0:T(512)S(1)}, f32[512]{0:T(512)}, u32[]{:S(2)}) copy-start(f32[512]{0:T(512)} %param.25) | copy-start | bytes 6148
  2.0 1.0 %copy-start.7 = (f32[1,3,128]{2,0,1:T(1,128)S(1)}, f32[1,3,128]{2,0,1:T(1,128)}, u32[]{:S(2)}) copy-start(f32[1,3,128]{2,0,1:T(1,128)} %param.19) | copy-start | bytes 4612
  2.0 1.0 %copy-start.8 = (f32[64]{0:T(128)S(1)}, f32[64]{0:T(128)}, u32[]{:S(2)}) copy-start(f32[64]{0:T(128)} %param.16) | copy-start | bytes 772
  2.0 1.0 %copy-start.9 = (s32[1,128,1]{1,2,0:T(1,128)S(1)}, s32[1,128,1]{1,2,0:T(1,128)}, u32[]{:S(2)}) copy-start(s32[1,128,1]{1,2,0:T(1,128)} %param.17) | copy-start | bytes 1540
  2.0 1.0 %copy-start.10 = (s32[1,128]{1,0:T(1,128)S(1)}, s32[1,128]{1,0:T(1,128)}, u32[]{:S(2)}) copy-start(s32[1,128]{1,0:T(1,128)} %cell_ref.1) | copy-start | bytes 1540
  2.0 1.0 %copy-start.11 = (f32[5]{0:T(128)S(1)}, f32[5]{0:T(128)}, u32[]{:S(2)}) copy-start(f32[5]{0:T(128)} %param.27) | copy-start | bytes 64

commit v4 on v3

--- a/solution.py
+++ b/solution.py
@@ -15,7 +15,7 @@
 
 MESH = pl.DeviceIdType.MESH
 PLANES = 10
-GROUPS = ((0, 6), (6, 4))
+GROUPS = ((0, 2), (2, 4), (6, 4))
 f32 = jnp.float32
 bf16 = jnp.bfloat16
 
@@ -65,7 +65,7 @@
 
 def encode_part(place, refs, scratch, prepare):
     z, tile, n_tile, others = place
-    fields_ref, weight_ref, conv_bias_ref, owner_ref, cell_ref, frac_ref = refs
+    fields_ref, weight_copy, weight_ref, conv_bias_ref, owner_ref, cell_ref, frac_ref = refs
     (
         halo, taps, partial, latent, corner, asked, wanted, answer, answered,
         halo_send, halo_recv, ask_send, ask_recv, answer_send, answer_recv,
@@ -171,6 +171,7 @@
         position_of(cell % 128, 2, 128),
     ]
 
+    weight_copy.wait()
     turned = jnp.transpose(weight_ref[...].astype(f32)).astype(bf16)
     for dx in range(3):
         for y_in in range(4):
@@ -192,7 +193,7 @@
             [
                 plane[:, column * 128 : (column + 1) * 128]
                 for plane in planes
-                for column in (pair, (pair + 1) % 4)
+                for column in ((pair + 3) % 4, pair)
             ],
             axis=1,
         )
@@ -225,8 +226,8 @@
     for y in range(8):
         weight_y = side(base_y, y, 8, part[1])
         for p in range(5):
-            start = (p * 4 + y // 2) * 128
-            corner[y % 2, :, start : start + 128] = ((weight_x[p] * weight_y) * weight_z).astype(bf16)
+            start = (p * 4 + (y + 1) // 2 % 4) * 128
+            corner[1 - y % 2, :, start : start + 128] = ((weight_x[p] * weight_y) * weight_z).astype(bf16)
 
     conv_bias = jnp.concatenate([conv_bias_ref[...], conv_bias_ref[...]], axis=1)
     arrived = set()
@@ -247,9 +248,9 @@
             v = 0.5 * v * (1.0 + jnp.tanh(GELU_SCALE * (v + 0.044715 * (v * v * v))))
             latent[(p * 4 + pair) * 128 : (p * 4 + pair + 1) * 128] = v.astype(bf16)
 
-    even = jnp.dot(corner[0], latent[...], preferred_element_type=f32)
-    odd = jnp.dot(corner[1], latent[...], preferred_element_type=f32)
-    answer[...] = (even + pltpu.roll(odd, 64, axis=1)).astype(bf16).astype(f32)
+    left_half = jnp.dot(corner[0], latent[...], preferred_element_type=f32)
+    right_half = jnp.dot(corner[1], latent[...], preferred_element_type=f32)
+    answer[...] = (left_half + pltpu.roll(right_half, 64, axis=1)).astype(bf16).astype(f32)
     exchange(answer, answered, answer_send, answer_recv)()
     interp = jnp.dot(from_slots, answered[...].astype(bf16), preferred_element_type=f32)
     return interp[:, :64].astype(bf16), position
@@ -261,14 +262,14 @@
     target_ref, w_latent_ref, w_pos_ref, bias_one_ref, w_mid_ref,
     bias_two_ref, w_out_ref, bias_out_ref,
     prediction_ref, packed_ref,
-    grads, pair_buf, plane_buf, z_send_0, z_send_1, z_buf_0, z_buf_1, z_all_0, z_all_1, piece,
-    act_high, act_low, cot_high, cot_low,
+    grads, pair_buf, plane_buf, z_send_0, z_send_1, z_send_2, z_buf_0, z_buf_1, z_buf_2, z_all_0, z_all_1, z_all_2, piece,
+    act_high, act_low, cot_high, cot_low, mixing,
     pair_send, pair_recv, plane_send, plane_recv, zs_send, zs_recv, zg_send, zg_recv,
     pg_send, pg_recv, cg_send, cg_recv,
-    w_mid_buf, w_mid_sem, mid_high, mid_low, turned_high, turned_low,
+    weight_buf, weight_sem, w_mid_buf, w_mid_sem, mid_high, mid_low, turned_high, turned_low,
     *encode_scratch,
 ):
-    z_send, z_buf, z_all = (z_send_0, z_send_1), (z_buf_0, z_buf_1), (z_all_0, z_all_1)
+    z_send, z_buf, z_all = (z_send_0, z_send_1, z_send_2), (z_buf_0, z_buf_1, z_buf_2), (z_all_0, z_all_1, z_all_2)
     n_z, n_tile, query_total = sizes
     n_xy = n_tile // 2
     rows_xy = 128 // n_xy
@@ -290,6 +291,8 @@
     tiles = [chip_index * 2 + side for chip_index in chips for side in (core, other)] + [chip * 2 + other]
     w_mid_copy = pltpu.make_async_copy(w_mid_ref, w_mid_buf, w_mid_sem)
     w_mid_copy.start()
+    weight_copy = pltpu.make_async_copy(weight_ref, weight_buf, weight_sem)
+    weight_copy.start()
     barrier = pltpu.get_barrier_semaphore()
     for index in tiles:
         pl.semaphore_signal(barrier, inc=1, device_id={"replica": z, "tile": index}, device_id_type=MESH)
@@ -303,7 +306,7 @@
 
     latent_rows, position = encode_part(
         (z, tile, n_tile, tiles),
-        (fields_ref, weight_ref, conv_bias_ref, owner_ref, cell_ref, frac_ref),
+        (fields_ref, weight_copy, weight_buf, conv_bias_ref, owner_ref, cell_ref, frac_ref),
         encode_scratch,
         prepare,
     )
@@ -330,9 +333,10 @@
     keep(act_high, act_low, 4, curve_one * pos_square)
     w_mid = (mid_high[...], mid_low[...])
 
+    mixing[...] = product((act_high[...], act_low[...]), w_mid, NN)
+
     def mixed(k):
-        rows = slice(k * 128, (k + 1) * 128)
-        return product((act_high[rows], act_low[rows]), w_mid, NN)
+        return mixing[k * 128 : (k + 1) * 128]
 
     act_two = jnp.tanh(mixed(0) + bias_two_ref[...])
     slope_two = 1.0 - act_two * act_two
@@ -427,9 +431,10 @@
     keep(cot_high, cot_low, 0, d_sum_two)
     grad_bias_two = jnp.sum(d_sum_two, axis=0, keepdims=True)
 
+    mixing[...] = product((cot_high[...], cot_low[...]), (turned_high[...], turned_low[...]), NN)
+
     def back(k):
-        rows = slice(k * 128, (k + 1) * 128)
-        return product((cot_high[rows], cot_low[rows]), (turned_high[...], turned_low[...]), NN)
+        return mixing[k * 128 : (k + 1) * 128]
 
     d_act_one = back(0)
     d_slope_one = jnp.zeros_like(slope_one)
@@ -479,15 +484,6 @@
 
     pair_copies = [pair_copy(0, 2, 2), pair_copy(2, 4, 0), pair_copy(6, 4, 1)]
     pair_copies[0].start()
-
-    for half in range(2):
-        r = half * 256
-        block = product(
-            (act_high[:, r : r + 256], act_low[:, r : r + 256]), (cot_high[...], cot_low[...]), TN
-        )
-        for k in range(4):
-            grads[2 + half * 4 + k] = block[:, k * 128 : (k + 1) * 128]
-        pair_copies[1 + half].start()
 
     mine = pl.ds(pl.multiple_of(core * 128, 128), 128)
 
@@ -582,23 +578,30 @@
         copy.start()
         return copy
 
-    pair_copies[0].wait()
-    pair_sum((0, 1))
-    pair_copies[1].wait()
-    pair_sum((2, 3, 4, 5))
-    start_plane_sum(0)
+    for half in range(2):
+        r = half * 256
+        block = product(
+            (act_high[:, r : r + 256], act_low[:, r : r + 256]), (cot_high[...], cot_low[...]), TN
+        )
+        for k in range(4):
+            grads[2 + half * 4 + k] = block[:, k * 128 : (k + 1) * 128]
+        pair_copies[1 + half].start()
+        pair_copies[half].wait()
+        pair_sum(range(*((0, 2) if half == 0 else (2, 6))))
+        start_plane_sum(half)
     pair_copies[2].wait()
-    pair_sum((6, 7, 8, 9))
-    start_plane_sum(1)
-    plane_sum(0)
-    start_z_sum(0)
-    plane_sum(1)
-    start_z_sum(1)
+    pair_sum(range(6, 10))
+    start_plane_sum(2)
+    for group in range(3):
+        plane_sum(group)
+        start_z_sum(group)
     z_sum(0)
     z_sum(1)
     start_gather(0)
+    z_sum(2)
     start_gather(1)
-    crossed = [cross(0), cross(1)]
+    start_gather(2)
+    crossed = [cross(group) for group in range(3)]
     for copy in crossed:
         copy.wait()
 
@@ -619,30 +622,36 @@
             jax.ShapeDtypeStruct((PLANES, 256, 128), f32),
         ),
         in_specs=[
-            pl.BlockSpec(memory_space=pltpu.HBM if k == 10 else pltpu.VMEM) for k in range(14)
+            pl.BlockSpec(memory_space=pltpu.HBM if k in (1, 10) else pltpu.VMEM) for k in range(14)
         ],
         out_specs=[pl.BlockSpec(memory_space=pltpu.VMEM)] * 2,
         scratch_shapes=[
             pltpu.VMEM((PLANES, 256, 128), f32),
             pltpu.VMEM((PLANES, 128, 128), f32),
             pltpu.VMEM((n_xy, PLANES, rows_xy, 128), f32),
-            pltpu.VMEM((n_z, 6 * rows_z, 128), f32),
+            pltpu.VMEM((n_z, 2 * rows_z, 128), f32),
             pltpu.VMEM((n_z, 4 * rows_z, 128), f32),
-            pltpu.VMEM((n_z, 6 * rows_z, 128), f32),
             pltpu.VMEM((n_z, 4 * rows_z, 128), f32),
-            pltpu.VMEM((n_z, 6 * rows_z, 128), f32),
+            pltpu.VMEM((n_z, 2 * rows_z, 128), f32),
+            pltpu.VMEM((n_z, 4 * rows_z, 128), f32),
+            pltpu.VMEM((n_z, 4 * rows_z, 128), f32),
+            pltpu.VMEM((n_z, 2 * rows_z, 128), f32),
+            pltpu.VMEM((n_z, 4 * rows_z, 128), f32),
             pltpu.VMEM((n_z, 4 * rows_z, 128), f32),
             pltpu.VMEM((PLANES, rows_xy, 128), f32),
             pltpu.VMEM((640, hidden), bf16),
             pltpu.VMEM((640, hidden), bf16),
             pltpu.VMEM((640, hidden), bf16),
             pltpu.VMEM((640, hidden), bf16),
+            pltpu.VMEM((640, hidden), f32),
             DMA((3,)), DMA((3,)),
-            DMA((2,)), DMA((2,)),
-            DMA((2,)), DMA((2,)),
-            DMA((2,)), DMA((2,)),
-            DMA((2,)), DMA((2,)),
-            DMA((2,)), DMA((2,)),
+            DMA((3,)), DMA((3,)),
+            DMA((3,)), DMA((3,)),
+            DMA((3,)), DMA((3,)),
+            DMA((3,)), DMA((3,)),
+            DMA((3,)), DMA((3,)),
+            pltpu.VMEM((64, 1728), bf16),
+            DMA(()),
             pltpu.VMEM((hidden, hidden), f32),
             DMA(()),
             pltpu.VMEM((hidden, hidden), bf16),
@@ -667,7 +676,7 @@
         ),
         name="step",
     )(
-        fields, weight, conv_bias.reshape(1, -1), owner, cell, frac, target, w_latent, w_pos, bias_one.reshape(1, -1),
+        fields, pltpu.with_memory_space_constraint(weight, pltpu.HBM), conv_bias.reshape(1, -1), owner, cell, frac, target, w_latent, w_pos, bias_one.reshape(1, -1),
         pltpu.with_memory_space_constraint(w_mid, pltpu.HBM),
         bias_two.reshape(1, -1), w_out, bias_out.reshape(1, -1),
     )
@@ -736,7 +745,7 @@
     tile_count = lax.axis_size("tile")
     replica_count = lax.axis_size("replica")
     channels, planes, rows_y, rows_z = fields.shape[1:]
-    turned = jnp.transpose(jnp.roll(fields[0], 1, axis=2), (1, 3, 2, 0))
+    turned = jnp.transpose(fields[0], (1, 3, 2, 0))
     turned = turned.reshape(planes, rows_z, rows_y * channels)
     query_count = query_cell.shape[1]
     query_total = float(query_count * tile_count * replica_count)

time: 63.5 us -> 62.3 us (0.981)
  Pallas kernels: 60.4 us -> 59.7 us
    unnamed x25 -> x23, local copies, waits for them, and re-layouts: 1.87 us -> 1.4 us
where the time goes in v4:
time: 62.3 us; the launch traced here: 62.2 us
  Pallas kernels  59.7 us (96%)
  local copies, waits for them, and re-layouts  1.63 us (3%)
  between operations  0.84 us (1%)
    pallas_call x1, Pallas kernels, whole_step(): pl.pallas_call(functools.partial(step_kernel, sizes), out_shape=(jax.Shap...  58 us
    pallas_call x1, Pallas kernels, unpacked(): pl.pallas_call(unpack_kernel, out_shape=tuple((jax.ShapeDtypeStruct(shape...  1.7 us
    unnamed x23, local copies, waits for them, and re-layouts  1.4 us

profile of v4, /device:TPU:1, one launch (start us, length us, event | category | flops | bytes accessed | tf_op | source)
XLA Modules:
  0.0 62.2 jit_solution(17357832535439881616)
XLA Ops:
  0.6 0.0 copy-start.10
  0.7 0.0 copy-start.1
  0.7 0.0 copy-start.5
  0.7 0.0 copy-start.4
  0.7 0.0 copy-start.2
  0.7 0.0 copy-start
  0.7 0.0 copy-start.3
  0.7 0.0 copy-start.6
  0.7 0.0 copy-start.9
  0.7 0.0 copy-start.8
  0.7 0.0 copy-start.7
  0.8 1.4 %copy.24 = bf16[1,64,4,8,128]{4,1,3,2,0:T(8,128)(2,1)S(1)} copy(bf16[1,64,4,8,128]{4,3,2,1,0:T(8,128)(2,1)} %param.14) | data formatting | bytes 1048576 | tf_op args[0]
  2.1 0.2 copy.25.fields_ref
  2.3 0.0 copy-done.10
  2.4 0.0 copy-done.1
  2.4 0.0 copy-done.5
  2.4 0.0 copy-done.4
  2.4 0.0 copy-done.2
  2.4 0.0 copy-done
  2.4 0.0 copy-done.3
  2.4 0.0 copy-done.6
  2.4 0.0 copy-done.9
  2.4 0.0 copy-done.8
  2.4 0.0 copy-done.7
  2.5 58.0 %step.1 = (f32[5,1,128]{2,1,0:T(1,128)S(1)}, f32[10,256,128]{2,1,0:T(8,128)S(1)}) custom-call(bf16[4,128,512]{2,1,0:T(8,128)(2,1)S(1)} %copy.25.fields_ref, bf16[64,1728]{1,0:T(8,128)(2,1)} %weight_ref.1, f32[1,64]{1,0:T(1,128)S(1)} %bitcast.21, s32[1,128]{1,0:T(1,128)S(1)} %bitcast.22, s32[1,128]{1,0:T(1,128)S(1)} %copy-done.9, f32[3,1,128]{2,1,0:T(1,128)S(1)} %bitcast.20, ...), custom_call_target="tpu_custom_call" | custom-call | tf_op jit(solution)/shard_map/step/pallas_call | solution.py:618
  60.5 1.7 %unpack.1 = (f32[5,1,128]{2,1,0:T(1,128)}, f32[64,512]{1,0:T(8,128)}, f32[3,512]{1,0:T(4,128)}, f32[1,512]{1,0:T(1,128)}, f32[512,512]{1,0:T(8,128)}, /*index=5*...) custom-call(f32[5,1,128]{2,1,0:T(1,128)S(1)} %get-tuple-element.20.prediction_ref, ...), custom_call_target="tpu_custom_call" | custom-call | tf_op jit(solution)/shard_map/unpack/pallas_call | solution.py:717
Async XLA Ops:
  0.6 1.7 %copy-start.10 = (f32[5]{0:T(128)S(1)}, f32[5]{0:T(128)}, u32[]{:S(2)}) copy-start(f32[5]{0:T(128)} %param.27) | copy-start | bytes 64
  0.7 1.7 %copy-start.1 = (f32[5,512]{1,0:T(8,128)S(1)}, f32[5,512]{1,0:T(8,128)}, u32[]{:S(2)}) copy-start(f32[5,512]{1,0:T(8,128)} %w_out_ref.1) | copy-start | bytes 30724
  0.7 1.7 %copy-start.5 = (f32[512]{0:T(512)S(1)}, f32[512]{0:T(512)}, u32[]{:S(2)}) copy-start(f32[512]{0:T(512)} %param.25) | copy-start | bytes 6148
  0.7 1.7 %copy-start.4 = (f32[512]{0:T(512)S(1)}, f32[512]{0:T(512)}, u32[]{:S(2)}) copy-start(f32[512]{0:T(512)} %param.23) | copy-start | bytes 6148
  0.7 1.7 %copy-start.2 = (f32[3,512]{1,0:T(4,128)S(1)}, f32[3,512]{1,0:T(4,128)}, u32[]{:S(2)}) copy-start(f32[3,512]{1,0:T(4,128)} %w_pos_ref.1) | copy-start | bytes 18436
  0.7 1.7 %copy-start = (f32[64,512]{1,0:T(8,128)S(1)}, f32[64,512]{1,0:T(8,128)}, u32[]{:S(2)}) copy-start(f32[64,512]{1,0:T(8,128)} %w_latent_ref.1) | copy-start | bytes 393220
  0.7 1.7 %copy-start.3 = (f32[1,5,128]{2,0,1:T(1,128)S(1)}, f32[1,5,128]{2,0,1:T(1,128)}, u32[]{:S(2)}) copy-start(f32[1,5,128]{2,0,1:T(1,128)} %param.20) | copy-start | bytes 7684
  0.7 1.7 %copy-start.6 = (f32[1,3,128]{2,0,1:T(1,128)S(1)}, f32[1,3,128]{2,0,1:T(1,128)}, u32[]{:S(2)}) copy-start(f32[1,3,128]{2,0,1:T(1,128)} %param.19) | copy-start | bytes 4612
  0.7 1.7 %copy-start.9 = (s32[1,128]{1,0:T(1,128)S(1)}, s32[1,128]{1,0:T(1,128)}, u32[]{:S(2)}) copy-start(s32[1,128]{1,0:T(1,128)} %cell_ref.1) | copy-start | bytes 1540
  0.7 1.7 %copy-start.8 = (s32[1,128,1]{1,2,0:T(1,128)S(1)}, s32[1,128,1]{1,2,0:T(1,128)}, u32[]{:S(2)}) copy-start(s32[1,128,1]{1,2,0:T(1,128)} %param.17) | copy-start | bytes 1540
  0.7 1.7 %copy-start.7 = (f32[64]{0:T(128)S(1)}, f32[64]{0:T(128)}, u32[]{:S(2)}) copy-start(f32[64]{0:T(128)} %param.16) | copy-start | bytes 772

commit v5 on v4

--- a/solution.py
+++ b/solution.py
@@ -162,15 +162,6 @@
     for copy in halo_copies.values():
         copy.start()
 
-    def position_of(base, d, span):
-        return as_column((base.astype(f32) + fraction[d : d + 1]) * (1.0 / span))
-
-    position = [
-        position_of(owner_ref[...] * 4 + cell // 1024, 0, 4 * n_tile),
-        position_of(cell // 128 % 8, 1, 8),
-        position_of(cell % 128, 2, 128),
-    ]
-
     weight_copy.wait()
     turned = jnp.transpose(weight_ref[...].astype(f32)).astype(bf16)
     for dx in range(3):
@@ -203,7 +194,6 @@
         planes = [fields_ref[x] for x in own]
         for pair in range(4):
             partial[p * 4 + pair] = windowed(planes, pair, first)
-    prepare()
 
     asked_finish()
     table = asked[...]
@@ -251,7 +241,19 @@
     left_half = jnp.dot(corner[0], latent[...], preferred_element_type=f32)
     right_half = jnp.dot(corner[1], latent[...], preferred_element_type=f32)
     answer[...] = (left_half + pltpu.roll(right_half, 64, axis=1)).astype(bf16).astype(f32)
-    exchange(answer, answered, answer_send, answer_recv)()
+    answered_finish = exchange(answer, answered, answer_send, answer_recv)
+
+    def position_of(base, d, span):
+        return as_column((base.astype(f32) + fraction[d : d + 1]) * (1.0 / span))
+
+    position = [
+        position_of(owner_ref[...] * 4 + cell // 1024, 0, 4 * n_tile),
+        position_of(cell // 128 % 8, 1, 8),
+        position_of(cell % 128, 2, 128),
+    ]
+
+    prepare()
+    answered_finish()
     interp = jnp.dot(from_slots, answered[...].astype(bf16), preferred_element_type=f32)
     return interp[:, :64].astype(bf16), position
 

time: 62.3 us -> 62.3 us (level)
  no operation moved by 1% of the time
where the time goes in v5:
time: 62.3 us; the launch traced here: 62.2 us
  Pallas kernels  59.7 us (96%)
  local copies, waits for them, and re-layouts  1.63 us (3%)
  between operations  0.84 us (1%)
    pallas_call x1, Pallas kernels, whole_step(): pl.pallas_call(functools.partial(step_kernel, sizes), out_shape=(jax.Shap...  58 us
    pallas_call x1, Pallas kernels, unpacked(): pl.pallas_call(unpack_kernel, out_shape=tuple((jax.ShapeDtypeStruct(shape...  1.7 us
    unnamed x23, local copies, waits for them, and re-layouts  1.4 us

profile of v5, /device:TPU:1, one launch (start us, length us, event | category | flops | bytes accessed | tf_op | source)
XLA Modules:
  0.0 62.2 jit_solution(9902316681669139678)
XLA Ops:
  0.6 0.0 copy-start.10
  0.7 0.0 copy-start.1
  0.7 0.0 copy-start.5
  0.7 0.0 copy-start.4
  0.7 0.0 copy-start.2
  0.7 0.0 copy-start
  0.7 0.0 copy-start.3
  0.7 0.0 copy-start.6
  0.7 0.0 copy-start.9
  0.7 0.0 copy-start.8
  0.7 0.0 copy-start.7
  0.8 1.4 %copy.24 = bf16[1,64,4,8,128]{4,1,3,2,0:T(8,128)(2,1)S(1)} copy(bf16[1,64,4,8,128]{4,3,2,1,0:T(8,128)(2,1)} %param.14) | data formatting | bytes 1048576 | tf_op args[0]
  2.1 0.2 copy.25.fields_ref
  2.3 0.0 copy-done.10
  2.4 0.0 copy-done.1
  2.4 0.0 copy-done.5
  2.4 0.0 copy-done.4
  2.4 0.0 copy-done.2
  2.4 0.0 copy-done
  2.4 0.0 copy-done.3
  2.4 0.0 copy-done.6
  2.4 0.0 copy-done.9
  2.4 0.0 copy-done.8
  2.4 0.0 copy-done.7
  2.5 58.0 %step.1 = (f32[5,1,128]{2,1,0:T(1,128)S(1)}, f32[10,256,128]{2,1,0:T(8,128)S(1)}) custom-call(bf16[4,128,512]{2,1,0:T(8,128)(2,1)S(1)} %copy.25.fields_ref, bf16[64,1728]{1,0:T(8,128)(2,1)} %weight_ref.1, f32[1,64]{1,0:T(1,128)S(1)} %bitcast.21, s32[1,128]{1,0:T(1,128)S(1)} %bitcast.22, s32[1,128]{1,0:T(1,128)S(1)} %copy-done.9, f32[3,1,128]{2,1,0:T(1,128)S(1)} %bitcast.20, ...), custom_call_target="tpu_custom_call" | custom-call | tf_op jit(solution)/shard_map/step/pallas_call | solution.py:620
  60.5 1.7 %unpack.1 = (f32[5,1,128]{2,1,0:T(1,128)}, f32[64,512]{1,0:T(8,128)}, f32[3,512]{1,0:T(4,128)}, f32[1,512]{1,0:T(1,128)}, f32[512,512]{1,0:T(8,128)}, /*index=5*...) custom-call(f32[5,1,128]{2,1,0:T(1,128)S(1)} %get-tuple-element.20.prediction_ref, ...), custom_call_target="tpu_custom_call" | custom-call | tf_op jit(solution)/shard_map/unpack/pallas_call | solution.py:719
Async XLA Ops:
  0.6 1.7 %copy-start.10 = (f32[5]{0:T(128)S(1)}, f32[5]{0:T(128)}, u32[]{:S(2)}) copy-start(f32[5]{0:T(128)} %param.27) | copy-start | bytes 64
  0.7 1.7 %copy-start.1 = (f32[5,512]{1,0:T(8,128)S(1)}, f32[5,512]{1,0:T(8,128)}, u32[]{:S(2)}) copy-start(f32[5,512]{1,0:T(8,128)} %w_out_ref.1) | copy-start | bytes 30724
  0.7 1.7 %copy-start.5 = (f32[512]{0:T(512)S(1)}, f32[512]{0:T(512)}, u32[]{:S(2)}) copy-start(f32[512]{0:T(512)} %param.25) | copy-start | bytes 6148
  0.7 1.7 %copy-start.4 = (f32[512]{0:T(512)S(1)}, f32[512]{0:T(512)}, u32[]{:S(2)}) copy-start(f32[512]{0:T(512)} %param.23) | copy-start | bytes 6148
  0.7 1.7 %copy-start.2 = (f32[3,512]{1,0:T(4,128)S(1)}, f32[3,512]{1,0:T(4,128)}, u32[]{:S(2)}) copy-start(f32[3,512]{1,0:T(4,128)} %w_pos_ref.1) | copy-start | bytes 18436
  0.7 1.7 %copy-start = (f32[64,512]{1,0:T(8,128)S(1)}, f32[64,512]{1,0:T(8,128)}, u32[]{:S(2)}) copy-start(f32[64,512]{1,0:T(8,128)} %w_latent_ref.1) | copy-start | bytes 393220
  0.7 1.7 %copy-start.3 = (f32[1,5,128]{2,0,1:T(1,128)S(1)}, f32[1,5,128]{2,0,1:T(1,128)}, u32[]{:S(2)}) copy-start(f32[1,5,128]{2,0,1:T(1,128)} %param.20) | copy-start | bytes 7684
  0.7 1.7 %copy-start.6 = (f32[1,3,128]{2,0,1:T(1,128)S(1)}, f32[1,3,128]{2,0,1:T(1,128)}, u32[]{:S(2)}) copy-start(f32[1,3,128]{2,0,1:T(1,128)} %param.19) | copy-start | bytes 4612
  0.7 1.7 %copy-start.9 = (s32[1,128]{1,0:T(1,128)S(1)}, s32[1,128]{1,0:T(1,128)}, u32[]{:S(2)}) copy-start(s32[1,128]{1,0:T(1,128)} %cell_ref.1) | copy-start | bytes 1540
  0.7 1.7 %copy-start.8 = (s32[1,128,1]{1,2,0:T(1,128)S(1)}, s32[1,128,1]{1,2,0:T(1,128)}, u32[]{:S(2)}) copy-start(s32[1,128,1]{1,2,0:T(1,128)} %param.17) | copy-start | bytes 1540
  0.7 1.7 %copy-start.7 = (f32[64]{0:T(128)S(1)}, f32[64]{0:T(128)}, u32[]{:S(2)}) copy-start(f32[64]{0:T(128)} %param.16) | copy-start | bytes 772
